TPU v7x, 512 devices: a whole 4x8x8 slice. The times are simulated.
512 devices in a mesh: ctx: 256 (over z, y, x), tp: 2 (over core).
Axes of the slice: x: 4, y: 8, z: 8, core: 2. Of those that a mesh axis runs over, the one named last changes fastest.
Arguments:
- queries: bfloat16 [32768, 64, 128], P(('ctx', 'tp')), may hold values from -24 to 24
- rotated_key_rows: bfloat16 [32768, 8, 128], P(('ctx', 'tp')), may hold values from -24 to 24
- unscaled_value_rows: bfloat16 [32768, 8, 128], P(('ctx', 'tp')), may hold values from -6 to 6
- key_block_scales: bfloat16 [256, 8], P('ctx', 'tp'), may hold values from 0.5 to 2
- value_block_scales: bfloat16 [256, 8], P('ctx', 'tp'), may hold values from 0.5 to 2
- doc_lengths: int32 [256], replicated, may hold values from 1 to 512, 32768 in all
Outputs:
- attended: bfloat16 [32768, 64, 128], P(('ctx', 'tp'))
Inputs may be any that keep to these rules, and one draw needn't show every extreme that they name: `doc_lengths`: they sum to 32768; the longest is exactly 512.
All inputs are finite; a program needn't handle non-finite values.
Results may differ from a plain program's by a relative error of at most 0.0035.
Values may be sent and summed in bfloat16 or wider, within the bound.
A program may use at most 64 MiB of HBM per device.

v0:
```python
import math

import jax
import jax.numpy as jnp
from jax import lax
from jax.sharding import PartitionSpec as P


def passed_along(value, axis, steps):
    count = lax.axis_size(axis)
    leading, last = (max(0, -steps), min(count, count - steps))
    return lax.ppermute(value, axis, [(source, source + steps) for source in range(leading, last)])


def document_of(positions, ends):
    return jnp.sum((positions[:, None] >= ends[None, :]).astype(jnp.int32), axis=1)


def shards(
    queries,
    rotated_key_rows,
    unscaled_value_rows,
    key_block_scales,
    value_block_scales,
    doc_lengths,
):
    query_rows, key_vectors, value_vectors = (
        lax.all_to_all(queries, "tp", split_axis=1, concat_axis=0, tiled=True),
        lax.all_to_all(rotated_key_rows, "tp", split_axis=1, concat_axis=0, tiled=True),
        lax.all_to_all(unscaled_value_rows, "tp", split_axis=1, concat_axis=0, tiled=True),
    )
    tokens_here = query_rows.shape[0]
    kv_local = key_vectors.shape[1]
    heads_local = query_rows.shape[1]
    query_group = heads_local // kv_local
    head_size = query_rows.shape[2]
    block_index = tokens_here // key_block_scales.shape[0]
    key_scale = jnp.repeat(key_block_scales, block_index, axis=0)
    value_scale = jnp.repeat(value_block_scales, block_index, axis=0)
    here = lax.axis_index("ctx")
    base = here * tokens_here
    ends = jnp.cumsum(doc_lengths)
    offsets = jnp.arange(tokens_here, dtype=jnp.int32)
    q_pos = base + offsets
    q_doc = document_of(q_pos, ends)
    grouped = query_rows.reshape(tokens_here, kv_local, query_group, head_size)
    reach = min(4, lax.axis_size("ctx") // 2)

    def attend(carry, pieces, back):
        k_part, v_part, k_scl, v_scl = pieces
        k_pos = base - back * tokens_here + offsets
        k_doc = document_of(k_pos, ends)
        allowed = (
            (k_doc[None, :] == q_doc[:, None])
            & (k_pos[None, :] <= q_pos[:, None])
            & (k_pos[None, :] >= 0)
        )
        mask_four = allowed[:, None, None, :]
        top, total, summed = carry
        scores = jnp.einsum("qkgd,jkd->qkgj", grouped, k_part, preferred_element_type=jnp.float32)
        scores = scores / math.sqrt(head_size) * k_scl.astype(jnp.float32).T[None, :, None, :]
        scores = jnp.where(mask_four, scores, -1e30)
        new_top = jnp.maximum(top, jnp.max(scores, axis=3))
        factor = jnp.exp(top - new_top)
        expo = jnp.where(mask_four, jnp.exp(scores - new_top[..., None]), 0.0)
        new_total = total * factor + jnp.sum(expo, axis=3)
        weights = (expo * v_scl.astype(jnp.float32).T[None, :, None, :]).astype(jnp.bfloat16)
        added = jnp.einsum("qkgj,jkd->qkgd", weights, v_part, preferred_element_type=jnp.float32)
        return (new_top, new_total, summed * factor[..., None] + added)

    carry = (
        jnp.full((tokens_here, kv_local, query_group), -1e30, jnp.float32),
        jnp.zeros((tokens_here, kv_local, query_group), jnp.float32),
        jnp.zeros((tokens_here, kv_local, query_group, head_size), jnp.float32),
    )
    local_part = (key_vectors, value_vectors, key_scale, value_scale)
    carry = attend(carry, local_part, 0)
    moving = local_part
    for back in range(1, reach + 1):
        moving = passed_along((moving[0], moving[1], moving[2], moving[3]), "ctx", 1)
        carry = attend(carry, moving, back)
    top, total, summed = carry
    result = (
        (summed / total[..., None])
        .reshape(tokens_here, heads_local, head_size)
        .astype(jnp.bfloat16)
    )
    return lax.all_to_all(result, "tp", split_axis=0, concat_axis=1, tiled=True)


def solution(mesh):
    return jax.shard_map(
        shards,
        mesh=mesh,
        in_specs=(
            P(("ctx", "tp"), None, None),
            P(("ctx", "tp"), None, None),
            P(("ctx", "tp"), None, None),
            P("ctx", "tp"),
            P("ctx", "tp"),
            P(),
        ),
        out_specs=P(("ctx", "tp"), None, None),
        check_vma=False,
    )
```

profile of v0, /device:TPU:257, one launch (start us, length us, event | category | flops | bytes accessed | tf_op | source)
XLA Modules:
  0.0 125.9 jit_solution(6748612150527657303)
XLA Ops:
  0.7 3.1 %collective-permute-start.1 = (bf16[128,4]{0,1:T(4,128)(2,1)S(1)}, bf16[128,4]{0,1:T(4,128)(2,1)S(1)}, u32[]{:S(2)}, u32[]{:S(2)}) collective-permute-start(bf16[128,4]{0,1:T(4,128)(2,1)S(1)} %reshape.501), channel_id=1, source_target_pairs={{0,2},{2,4},{4,6},{6,8},{8,10},{10,12},{12,14},{14,16},{16,18},{18... | collective-permute-start | bytes 3080 | tf_op jit(solution)/shard_map/ppermute | solution.py:12
  4.8 4.4 %all_to_all.69 = bf16[64,8,128]{2,0,1:T(8,128)(2,1)S(1)} all-to-all(bf16[64,8,128]{2,0,1:T(8,128)(2,1)S(1)} %copy.38), channel_id=1, replica_groups=mesh['ctx'=256,'tp'=2] {'tp'}, dimensions={1} | all-to-all | bytes 262144 | tf_op jit(solution)/shard_map/all_to_all | solution.py:29
  9.2 3.1 %collective-permute-start = (bf16[128,4,128]{2,0,1:T(8,128)(2,1)S(1)}, bf16[128,4,128]{2,0,1:T(8,128)(2,1)S(1)}, u32[]{:S(2)}, u32[]{:S(2)}) collective-permute-start(bf16[128,4,128]{2,0,1:T(8,128)(2,1)S(1)} %bitcast.196), channel_id=1, source_target_pairs={{0,2},{2,4},{4,6},{6,8},{8,10},{10,12},{12,14},{14,16},{16,18},{18... | collective-permute-start | bytes 393224 | tf_op jit(solution)/shard_map/ppermute | solution.py:12
  13.9 4.0 %all-to-all-start.2 = ((bf16[64,8,128]{2,0,1:T(8,128)(2,1)}), bf16[64,8,128]{2,0,1:T(8,128)(2,1)S(1)}, u32[]{:S(2)}, u32[]{:S(2)}) async-start(bf16[64,8,128]{2,0,1:T(8,128)(2,1)} %copy.42), calls=%async_computation.2 | async-start | bytes 262144 | tf_op jit(solution)/shard_map/all_to_all | solution.py:30
  17.9 2.9 %copy.40 = bf16[64,64,128]{2,0,1:T(8,128)(2,1)} copy(bf16[64,64,128]{2,1,0:T(8,128)(2,1)} %param.6) | data formatting | bytes 2097152 | tf_op args[0]
  20.8 3.6 %all-to-all-start.1 = ((bf16[64,64,128]{2,0,1:T(8,128)(2,1)}), bf16[64,64,128]{2,0,1:T(8,128)(2,1)S(1)}, u32[]{:S(2)}, u32[]{:S(2)}) async-start(bf16[64,64,128]{2,0,1:T(8,128)(2,1)} %copy.40), calls=%async_computation.1 | async-start | bytes 2097152 | tf_op jit(solution)/shard_map/all_to_all | solution.py:28
  24.4 2.8 %collective-permute-start.3 = (bf16[128,4,128]{2,0,1:T(8,128)(2,1)S(1)}, bf16[128,4,128]{2,0,1:T(8,128)(2,1)S(1)}, u32[]{:S(2)}, u32[]{:S(2)}) collective-permute-start(bf16[128,4,128]{2,0,1:T(8,128)(2,1)S(1)} %bitcast.200), channel_id=1, source_target_pairs={{0,2},{2,4},{4,6},{6,8},{8,10},{10,12},{12,14},{14,16},{16,18},{18... | collective-permute-start | bytes 393224 | tf_op jit(solution)/shard_map/ppermute | solution.py:12
  27.4 3.1 %collective-permute-start.2 = (bf16[128,4]{0,1:T(4,128)(2,1)S(1)}, bf16[128,4]{0,1:T(4,128)(2,1)S(1)}, u32[]{:S(2)}, u32[]{:S(2)}) collective-permute-start(bf16[128,4]{0,1:T(4,128)(2,1)S(1)} %reshape.502), channel_id=1, source_target_pairs={{0,2},{2,4},{4,6},{6,8},{8,10},{10,12},{12,14},{14,16},{16,18},{18... | collective-permute-start | bytes 3080 | tf_op jit(solution)/shard_map/ppermute | solution.py:12
  32.4 3.1 %collective-permute-start.5 = (bf16[128,4]{0,1:T(4,128)(2,1)S(1)}, bf16[128,4]{0,1:T(4,128)(2,1)S(1)}, u32[]{:S(2)}, u32[]{:S(2)}) collective-permute-start(bf16[128,4]{0,1:T(4,128)(2,1)S(1)} %collective-permute-done.1), channel_id=1, source_target_pairs={{0,2},{2,4},{4,6},{6,8},{8,10},{10,12},{12,14},{14,16},{16,18},{18... | collective-permute-start | bytes 3080 | tf_op jit(solution)/shard_map/ppermute | solution.py:12
  35.6 1.7 %collective-permute-done.2 = bf16[128,4]{0,1:T(4,128)(2,1)S(1)} collective-permute-done((bf16[128,4]{0,1:T(4,128)(2,1)S(1)}, bf16[128,4]{0,1:T(4,128)(2,1)S(1)}, u32[]{:S(2)}, u32[]{:S(2)}) %collective-permute-start.2) | collective-permute-done | bytes 1056 | tf_op jit(solution)/shard_map/ppermute | solution.py:12
  37.3 1.9 %collective-permute-start.6 = (bf16[128,4]{0,1:T(4,128)(2,1)S(1)}, bf16[128,4]{0,1:T(4,128)(2,1)S(1)}, u32[]{:S(2)}, u32[]{:S(2)}) collective-permute-start(bf16[128,4]{0,1:T(4,128)(2,1)S(1)} %collective-permute-done.2), channel_id=1, source_target_pairs={{0,2},{2,4},{4,6},{6,8},{8,10},{10,12},{12,14},{14,16},{16,18},{18... | collective-permute-start | bytes 3080 | tf_op jit(solution)/shard_map/ppermute | solution.py:12
  39.2 3.0 %collective-permute-done.5 = bf16[128,4]{0,1:T(4,128)(2,1)S(1)} collective-permute-done((bf16[128,4]{0,1:T(4,128)(2,1)S(1)}, bf16[128,4]{0,1:T(4,128)(2,1)S(1)}, u32[]{:S(2)}, u32[]{:S(2)}) %collective-permute-start.5) | collective-permute-done | bytes 1056 | tf_op jit(solution)/shard_map/ppermute | solution.py:12
  42.2 1.9 %collective-permute-start.9 = (bf16[128,4]{0,1:T(4,128)(2,1)S(1)}, bf16[128,4]{0,1:T(4,128)(2,1)S(1)}, u32[]{:S(2)}, u32[]{:S(2)}) collective-permute-start(bf16[128,4]{0,1:T(4,128)(2,1)S(1)} %collective-permute-done.5), channel_id=1, source_target_pairs={{0,2},{2,4},{4,6},{6,8},{8,10},{10,12},{12,14},{14,16},{16,18},{18... | collective-permute-start | bytes 3080 | tf_op jit(solution)/shard_map/ppermute | solution.py:12
  44.1 2.9 %collective-permute-done.6 = bf16[128,4]{0,1:T(4,128)(2,1)S(1)} collective-permute-done((bf16[128,4]{0,1:T(4,128)(2,1)S(1)}, bf16[128,4]{0,1:T(4,128)(2,1)S(1)}, u32[]{:S(2)}, u32[]{:S(2)}) %collective-permute-start.6) | collective-permute-done | bytes 1056 | tf_op jit(solution)/shard_map/ppermute | solution.py:12
  47.0 1.9 %collective-permute-start.10 = (bf16[128,4]{0,1:T(4,128)(2,1)S(1)}, bf16[128,4]{0,1:T(4,128)(2,1)S(1)}, u32[]{:S(2)}, u32[]{:S(2)}) collective-permute-start(bf16[128,4]{0,1:T(4,128)(2,1)S(1)} %collective-permute-done.6), channel_id=1, source_target_pairs={{0,2},{2,4},{4,6},{6,8},{8,10},{10,12},{12,14},{14,16},{16,18},{18... | collective-permute-start | bytes 3080 | tf_op jit(solution)/shard_map/ppermute | solution.py:12
  48.9 3.0 %collective-permute-done.9 = bf16[128,4]{0,1:T(4,128)(2,1)S(1)} collective-permute-done((bf16[128,4]{0,1:T(4,128)(2,1)S(1)}, bf16[128,4]{0,1:T(4,128)(2,1)S(1)}, u32[]{:S(2)}, u32[]{:S(2)}) %collective-permute-start.9) | collective-permute-done | bytes 1056 | tf_op jit(solution)/shard_map/ppermute | solution.py:12
  51.9 1.9 %collective-permute-start.13 = (bf16[128,4]{0,1:T(4,128)(2,1)S(1)}, bf16[128,4]{0,1:T(4,128)(2,1)S(1)}, u32[]{:S(2)}, u32[]{:S(2)}) collective-permute-start(bf16[128,4]{0,1:T(4,128)(2,1)S(1)} %collective-permute-done.9), channel_id=1, source_target_pairs={{0,2},{2,4},{4,6},{6,8},{8,10},{10,12},{12,14},{14,16},{16,18},{18... | collective-permute-start | bytes 3080 | tf_op jit(solution)/shard_map/ppermute | solution.py:12
  53.8 2.9 %collective-permute-done.10 = bf16[128,4]{0,1:T(4,128)(2,1)S(1)} collective-permute-done((bf16[128,4]{0,1:T(4,128)(2,1)S(1)}, bf16[128,4]{0,1:T(4,128)(2,1)S(1)}, u32[]{:S(2)}, u32[]{:S(2)}) %collective-permute-start.10) | collective-permute-done | bytes 1056 | tf_op jit(solution)/shard_map/ppermute | solution.py:12
  56.8 1.9 %collective-permute-start.14 = (bf16[128,4]{0,1:T(4,128)(2,1)S(1)}, bf16[128,4]{0,1:T(4,128)(2,1)S(1)}, u32[]{:S(2)}, u32[]{:S(2)}) collective-permute-start(bf16[128,4]{0,1:T(4,128)(2,1)S(1)} %collective-permute-done.10), channel_id=1, source_target_pairs={{0,2},{2,4},{4,6},{6,8},{8,10},{10,12},{12,14},{14,16},{16,18},{18... | collective-permute-start | bytes 3080 | tf_op jit(solution)/shard_map/ppermute | solution.py:12
  58.7 3.0 %collective-permute-done.13 = bf16[128,4]{0,1:T(4,128)(2,1)S(1)} collective-permute-done((bf16[128,4]{0,1:T(4,128)(2,1)S(1)}, bf16[128,4]{0,1:T(4,128)(2,1)S(1)}, u32[]{:S(2)}, u32[]{:S(2)}) %collective-permute-start.13) | collective-permute-done | bytes 1056 | tf_op jit(solution)/shard_map/ppermute | solution.py:12
  61.7 4.9 %collective-permute-done.14 = bf16[128,4]{0,1:T(4,128)(2,1)S(1)} collective-permute-done((bf16[128,4]{0,1:T(4,128)(2,1)S(1)}, bf16[128,4]{0,1:T(4,128)(2,1)S(1)}, u32[]{:S(2)}, u32[]{:S(2)}) %collective-permute-start.14) | collective-permute-done | bytes 1056 | tf_op jit(solution)/shard_map/ppermute | solution.py:12
  66.5 1.9 %collective-permute-start.4 = (bf16[128,4,128]{2,0,1:T(8,128)(2,1)S(1)}, bf16[128,4,128]{2,0,1:T(8,128)(2,1)S(1)}, u32[]{:S(2)}, u32[]{:S(2)}) collective-permute-start(bf16[128,4,128]{2,0,1:T(8,128)(2,1)S(1)} %collective-permute-done), channel_id=1, source_target_pairs={{0,2},{2,4},{4,6},{6,8},{8,10},{10,12},{12,14},{14,16},{16,18},{18... | collective-permute-start | bytes 393224 | tf_op jit(solution)/shard_map/ppermute | solution.py:12
  68.4 1.9 %collective-permute-start.7 = (bf16[128,4,128]{2,0,1:T(8,128)(2,1)S(1)}, bf16[128,4,128]{2,0,1:T(8,128)(2,1)S(1)}, u32[]{:S(2)}, u32[]{:S(2)}) collective-permute-start(bf16[128,4,128]{2,0,1:T(8,128)(2,1)S(1)} %collective-permute-done.3), channel_id=1, source_target_pairs={{0,2},{2,4},{4,6},{6,8},{8,10},{10,12},{12,14},{14,16},{16,18},{18... | collective-permute-start | bytes 393224 | tf_op jit(solution)/shard_map/ppermute | solution.py:12
  70.8 6.8 %collective-permute-done.4 = bf16[128,4,128]{2,0,1:T(8,128)(2,1)S(1)} collective-permute-done((bf16[128,4,128]{2,0,1:T(8,128)(2,1)S(1)}, bf16[128,4,128]{2,0,1:T(8,128)(2,1)S(1)}, u32[]{:S(2)}, u32[]{:S(2)}) %collective-permute-start.4) | collective-permute-done | bytes 131104 | tf_op jit(solution)/shard_map/ppermute | solution.py:12
  77.6 1.9 %collective-permute-start.8 = (bf16[128,4,128]{2,0,1:T(8,128)(2,1)S(1)}, bf16[128,4,128]{2,0,1:T(8,128)(2,1)S(1)}, u32[]{:S(2)}, u32[]{:S(2)}) collective-permute-start(bf16[128,4,128]{2,0,1:T(8,128)(2,1)S(1)} %collective-permute-done.4), channel_id=1, source_target_pairs={{0,2},{2,4},{4,6},{6,8},{8,10},{10,12},{12,14},{14,16},{16,18},{18... | collective-permute-start | bytes 393224 | tf_op jit(solution)/shard_map/ppermute | solution.py:12
  79.6 1.9 %collective-permute-start.11 = (bf16[128,4,128]{2,0,1:T(8,128)(2,1)S(1)}, bf16[128,4,128]{2,0,1:T(8,128)(2,1)S(1)}, u32[]{:S(2)}, u32[]{:S(2)}) collective-permute-start(bf16[128,4,128]{2,0,1:T(8,128)(2,1)S(1)} %collective-permute-done.7), channel_id=1, source_target_pairs={{0,2},{2,4},{4,6},{6,8},{8,10},{10,12},{12,14},{14,16},{16,18},{18... | collective-permute-start | bytes 393224 | tf_op jit(solution)/shard_map/ppermute | solution.py:12
  82.0 6.8 %collective-permute-done.8 = bf16[128,4,128]{2,0,1:T(8,128)(2,1)S(1)} collective-permute-done((bf16[128,4,128]{2,0,1:T(8,128)(2,1)S(1)}, bf16[128,4,128]{2,0,1:T(8,128)(2,1)S(1)}, u32[]{:S(2)}, u32[]{:S(2)}) %collective-permute-start.8) | collective-permute-done | bytes 131104 | tf_op jit(solution)/shard_map/ppermute | solution.py:12
  88.8 1.9 %collective-permute-start.12 = (bf16[128,4,128]{2,0,1:T(8,128)(2,1)S(1)}, bf16[128,4,128]{2,0,1:T(8,128)(2,1)S(1)}, u32[]{:S(2)}, u32[]{:S(2)}) collective-permute-start(bf16[128,4,128]{2,0,1:T(8,128)(2,1)S(1)} %collective-permute-done.8), channel_id=1, source_target_pairs={{0,2},{2,4},{4,6},{6,8},{8,10},{10,12},{12,14},{14,16},{16,18},{18... | collective-permute-start | bytes 393224 | tf_op jit(solution)/shard_map/ppermute | solution.py:12
  90.7 2.1 %collective-permute-start.15 = (bf16[128,4,128]{2,0,1:T(8,128)(2,1)S(1)}, bf16[128,4,128]{2,0,1:T(8,128)(2,1)S(1)}, u32[]{:S(2)}, u32[]{:S(2)}) collective-permute-start(bf16[128,4,128]{2,0,1:T(8,128)(2,1)S(1)} %collective-permute-done.11), channel_id=1, source_target_pairs={{0,2},{2,4},{4,6},{6,8},{8,10},{10,12},{12,14},{14,16},{16,18},{18... | collective-permute-start | bytes 393224 | tf_op jit(solution)/shard_map/ppermute | solution.py:12
  93.3 6.6 %collective-permute-done.12 = bf16[128,4,128]{2,0,1:T(8,128)(2,1)S(1)} collective-permute-done((bf16[128,4,128]{2,0,1:T(8,128)(2,1)S(1)}, bf16[128,4,128]{2,0,1:T(8,128)(2,1)S(1)}, u32[]{:S(2)}, u32[]{:S(2)}) %collective-permute-start.12) | collective-permute-done | bytes 131104 | tf_op jit(solution)/shard_map/ppermute | solution.py:12
  107.2 4.5 %fusion.1 = bf16[128,4,8,128]{3,0,2,1:T(8,128)(2,1)S(1)} fusion(f32[4,128,8,128]{3,1,2,0:T(8,128)S(1)} %fusion.19, f32[4,128,8,128]{3,1,2,0:T(8,128)S(1)} %fusion.18, f32[4,128,8,128]{3,1,2,0:T(8,128)S(1)} %fusion.17, f32[4,128,8,128]{3,1,2,0:T(8,128)S(1)} %fusion.16, f32[4,128,128,8]{2,1,3,0:T(8,128)S(1)} %get-tuple-element.27, ...), kind=kOutput, calls=%fused_computation.2 | convolution fusion | flops 143130624 | bytes 11800576 | tf_op jit(solution)/shard_map/qkgj,jkd->qkgd/dot_general | solution.py:68
  112.4 12.4 %all_to_all.70 = bf16[128,32,128]{2,1,0:T(8,128)(2,1)S(1)} all-to-all(bf16[128,32,128]{2,1,0:T(8,128)(2,1)S(1)} %copy.49), channel_id=1, replica_groups=mesh['ctx'=256,'tp'=2] {'tp'}, dimensions={0} | all-to-all | bytes 2097152 | tf_op jit(solution)/shard_map/all_to_all | solution.py:88
  (62 shorter events, 15.6 us)
Async XLA Ops:
  0.7 31.7 %collective-permute-start.1 = (bf16[128,4]{0,1:T(4,128)(2,1)S(1)}, bf16[128,4]{0,1:T(4,128)(2,1)S(1)}, u32[]{:S(2)}, u32[]{:S(2)}) collective-permute-start(bf16[128,4]{0,1:T(4,128)(2,1)S(1)} %reshape.501), channel_id=1, source_target_pairs={{0,2},{2,4},{4,6},{6,8},{8,10},{10,12},{12,14},{14,16},{16,18},{18... | collective-permute-start | bytes 3080 | tf_op jit(solution)/shard_map/ppermute | solution.py:12
  9.2 57.3 %collective-permute-start = (bf16[128,4,128]{2,0,1:T(8,128)(2,1)S(1)}, bf16[128,4,128]{2,0,1:T(8,128)(2,1)S(1)}, u32[]{:S(2)}, u32[]{:S(2)}) collective-permute-start(bf16[128,4,128]{2,0,1:T(8,128)(2,1)S(1)} %bitcast.196), channel_id=1, source_target_pairs={{0,2},{2,4},{4,6},{6,8},{8,10},{10,12},{12,14},{14,16},{16,18},{18... | collective-permute-start | bytes 393224 | tf_op jit(solution)/shard_map/ppermute | solution.py:12
  13.9 6.9 %all-to-all-start.2 = ((bf16[64,8,128]{2,0,1:T(8,128)(2,1)}), bf16[64,8,128]{2,0,1:T(8,128)(2,1)S(1)}, u32[]{:S(2)}, u32[]{:S(2)}) async-start(bf16[64,8,128]{2,0,1:T(8,128)(2,1)} %copy.42), calls=%async_computation.2 | async-start | bytes 262144 | tf_op jit(solution)/shard_map/all_to_all | solution.py:30
  17.9 9.4 %copy-start.2 = (bf16[1,4]{1,0:T(2,128)(2,1)S(1)}, bf16[1,4]{1,0:T(2,128)(2,1)}, u32[]{:S(2)}) copy-start(bf16[1,4]{1,0:T(2,128)(2,1)} %param.10) | copy-start | bytes 28
  17.9 12.7 %copy-start.1 = (bf16[1,4]{1,0:T(2,128)(2,1)S(1)}, bf16[1,4]{1,0:T(2,128)(2,1)}, u32[]{:S(2)}) copy-start(bf16[1,4]{1,0:T(2,128)(2,1)} %param.9) | copy-start | bytes 28
  17.9 12.7 %copy-start = (s32[256]{0:T(256)S(1)}, s32[256]{0:T(256)}, u32[]{:S(2)}) copy-start(s32[256]{0:T(256)} %param.11) | copy-start | bytes 3076
  20.8 10.4 %all-to-all-start.1 = ((bf16[64,64,128]{2,0,1:T(8,128)(2,1)}), bf16[64,64,128]{2,0,1:T(8,128)(2,1)S(1)}, u32[]{:S(2)}, u32[]{:S(2)}) async-start(bf16[64,64,128]{2,0,1:T(8,128)(2,1)} %copy.40), calls=%async_computation.1 | async-start | bytes 2097152 | tf_op jit(solution)/shard_map/all_to_all | solution.py:28
  24.4 44.0 %collective-permute-start.3 = (bf16[128,4,128]{2,0,1:T(8,128)(2,1)S(1)}, bf16[128,4,128]{2,0,1:T(8,128)(2,1)S(1)}, u32[]{:S(2)}, u32[]{:S(2)}) collective-permute-start(bf16[128,4,128]{2,0,1:T(8,128)(2,1)S(1)} %bitcast.200), channel_id=1, source_target_pairs={{0,2},{2,4},{4,6},{6,8},{8,10},{10,12},{12,14},{14,16},{16,18},{18... | collective-permute-start | bytes 393224 | tf_op jit(solution)/shard_map/ppermute | solution.py:12
  27.4 9.9 %collective-permute-start.2 = (bf16[128,4]{0,1:T(4,128)(2,1)S(1)}, bf16[128,4]{0,1:T(4,128)(2,1)S(1)}, u32[]{:S(2)}, u32[]{:S(2)}) collective-permute-start(bf16[128,4]{0,1:T(4,128)(2,1)S(1)} %reshape.502), channel_id=1, source_target_pairs={{0,2},{2,4},{4,6},{6,8},{8,10},{10,12},{12,14},{14,16},{16,18},{18... | collective-permute-start | bytes 3080 | tf_op jit(solution)/shard_map/ppermute | solution.py:12
  32.4 9.7 %collective-permute-start.5 = (bf16[128,4]{0,1:T(4,128)(2,1)S(1)}, bf16[128,4]{0,1:T(4,128)(2,1)S(1)}, u32[]{:S(2)}, u32[]{:S(2)}) collective-permute-start(bf16[128,4]{0,1:T(4,128)(2,1)S(1)} %collective-permute-done.1), channel_id=1, source_target_pairs={{0,2},{2,4},{4,6},{6,8},{8,10},{10,12},{12,14},{14,16},{16,18},{18... | collective-permute-start | bytes 3080 | tf_op jit(solution)/shard_map/ppermute | solution.py:12
  37.3 9.7 %collective-permute-start.6 = (bf16[128,4]{0,1:T(4,128)(2,1)S(1)}, bf16[128,4]{0,1:T(4,128)(2,1)S(1)}, u32[]{:S(2)}, u32[]{:S(2)}) collective-permute-start(bf16[128,4]{0,1:T(4,128)(2,1)S(1)} %collective-permute-done.2), channel_id=1, source_target_pairs={{0,2},{2,4},{4,6},{6,8},{8,10},{10,12},{12,14},{14,16},{16,18},{18... | collective-permute-start | bytes 3080 | tf_op jit(solution)/shard_map/ppermute | solution.py:12
  42.2 9.7 %collective-permute-start.9 = (bf16[128,4]{0,1:T(4,128)(2,1)S(1)}, bf16[128,4]{0,1:T(4,128)(2,1)S(1)}, u32[]{:S(2)}, u32[]{:S(2)}) collective-permute-start(bf16[128,4]{0,1:T(4,128)(2,1)S(1)} %collective-permute-done.5), channel_id=1, source_target_pairs={{0,2},{2,4},{4,6},{6,8},{8,10},{10,12},{12,14},{14,16},{16,18},{18... | collective-permute-start | bytes 3080 | tf_op jit(solution)/shard_map/ppermute | solution.py:12
  47.0 9.7 %collective-permute-start.10 = (bf16[128,4]{0,1:T(4,128)(2,1)S(1)}, bf16[128,4]{0,1:T(4,128)(2,1)S(1)}, u32[]{:S(2)}, u32[]{:S(2)}) collective-permute-start(bf16[128,4]{0,1:T(4,128)(2,1)S(1)} %collective-permute-done.6), channel_id=1, source_target_pairs={{0,2},{2,4},{4,6},{6,8},{8,10},{10,12},{12,14},{14,16},{16,18},{18... | collective-permute-start | bytes 3080 | tf_op jit(solution)/shard_map/ppermute | solution.py:12
  51.9 9.7 %collective-permute-start.13 = (bf16[128,4]{0,1:T(4,128)(2,1)S(1)}, bf16[128,4]{0,1:T(4,128)(2,1)S(1)}, u32[]{:S(2)}, u32[]{:S(2)}) collective-permute-start(bf16[128,4]{0,1:T(4,128)(2,1)S(1)} %collective-permute-done.9), channel_id=1, source_target_pairs={{0,2},{2,4},{4,6},{6,8},{8,10},{10,12},{12,14},{14,16},{16,18},{18... | collective-permute-start | bytes 3080 | tf_op jit(solution)/shard_map/ppermute | solution.py:12
  56.8 9.7 %collective-permute-start.14 = (bf16[128,4]{0,1:T(4,128)(2,1)S(1)}, bf16[128,4]{0,1:T(4,128)(2,1)S(1)}, u32[]{:S(2)}, u32[]{:S(2)}) collective-permute-start(bf16[128,4]{0,1:T(4,128)(2,1)S(1)} %collective-permute-done.10), channel_id=1, source_target_pairs={{0,2},{2,4},{4,6},{6,8},{8,10},{10,12},{12,14},{14,16},{16,18},{18... | collective-permute-start | bytes 3080 | tf_op jit(solution)/shard_map/ppermute | solution.py:12
  66.5 11.1 %collective-permute-start.4 = (bf16[128,4,128]{2,0,1:T(8,128)(2,1)S(1)}, bf16[128,4,128]{2,0,1:T(8,128)(2,1)S(1)}, u32[]{:S(2)}, u32[]{:S(2)}) collective-permute-start(bf16[128,4,128]{2,0,1:T(8,128)(2,1)S(1)} %collective-permute-done), channel_id=1, source_target_pairs={{0,2},{2,4},{4,6},{6,8},{8,10},{10,12},{12,14},{14,16},{16,18},{18... | collective-permute-start | bytes 393224 | tf_op jit(solution)/shard_map/ppermute | solution.py:12
  68.4 11.1 %collective-permute-start.7 = (bf16[128,4,128]{2,0,1:T(8,128)(2,1)S(1)}, bf16[128,4,128]{2,0,1:T(8,128)(2,1)S(1)}, u32[]{:S(2)}, u32[]{:S(2)}) collective-permute-start(bf16[128,4,128]{2,0,1:T(8,128)(2,1)S(1)} %collective-permute-done.3), channel_id=1, source_target_pairs={{0,2},{2,4},{4,6},{6,8},{8,10},{10,12},{12,14},{14,16},{16,18},{18... | collective-permute-start | bytes 393224 | tf_op jit(solution)/shard_map/ppermute | solution.py:12
  77.6 11.1 %collective-permute-start.8 = (bf16[128,4,128]{2,0,1:T(8,128)(2,1)S(1)}, bf16[128,4,128]{2,0,1:T(8,128)(2,1)S(1)}, u32[]{:S(2)}, u32[]{:S(2)}) collective-permute-start(bf16[128,4,128]{2,0,1:T(8,128)(2,1)S(1)} %collective-permute-done.4), channel_id=1, source_target_pairs={{0,2},{2,4},{4,6},{6,8},{8,10},{10,12},{12,14},{14,16},{16,18},{18... | collective-permute-start | bytes 393224 | tf_op jit(solution)/shard_map/ppermute | solution.py:12
  79.6 11.1 %collective-permute-start.11 = (bf16[128,4,128]{2,0,1:T(8,128)(2,1)S(1)}, bf16[128,4,128]{2,0,1:T(8,128)(2,1)S(1)}, u32[]{:S(2)}, u32[]{:S(2)}) collective-permute-start(bf16[128,4,128]{2,0,1:T(8,128)(2,1)S(1)} %collective-permute-done.7), channel_id=1, source_target_pairs={{0,2},{2,4},{4,6},{6,8},{8,10},{10,12},{12,14},{14,16},{16,18},{18... | collective-permute-start | bytes 393224 | tf_op jit(solution)/shard_map/ppermute | solution.py:12
  88.8 11.1 %collective-permute-start.12 = (bf16[128,4,128]{2,0,1:T(8,128)(2,1)S(1)}, bf16[128,4,128]{2,0,1:T(8,128)(2,1)S(1)}, u32[]{:S(2)}, u32[]{:S(2)}) collective-permute-start(bf16[128,4,128]{2,0,1:T(8,128)(2,1)S(1)} %collective-permute-done.8), channel_id=1, source_target_pairs={{0,2},{2,4},{4,6},{6,8},{8,10},{10,12},{12,14},{14,16},{16,18},{18... | collective-permute-start | bytes 393224 | tf_op jit(solution)/shard_map/ppermute | solution.py:12
  90.7 16.5 %collective-permute-start.15 = (bf16[128,4,128]{2,0,1:T(8,128)(2,1)S(1)}, bf16[128,4,128]{2,0,1:T(8,128)(2,1)S(1)}, u32[]{:S(2)}, u32[]{:S(2)}) collective-permute-start(bf16[128,4,128]{2,0,1:T(8,128)(2,1)S(1)} %collective-permute-done.11), channel_id=1, source_target_pairs={{0,2},{2,4},{4,6},{6,8},{8,10},{10,12},{12,14},{14,16},{16,18},{18... | collective-permute-start | bytes 393224 | tf_op jit(solution)/shard_map/ppermute | solution.py:12
where the time goes:
time: 127 us; the launch traced here: 126 us
  starting transfers between devices  44.1 us (35%)
  waiting for transfers between devices  41.6 us (33%)
  blocking collectives  16.8 us (13%)
  matrix products  10.4 us (8%)
  local copies, waits for them, and re-layouts  8.31 us (7%)
  other arithmetic  4.24 us (3%)
    ppermute x16, waiting for transfers between devices, passed_along(): lax.ppermute(value, axis, [(source, source + steps) for source in range(l...  41.6 us
    ppermute x16, starting transfers between devices, passed_along(): lax.ppermute(value, axis, [(source, source + steps) for source in range(l...  36.5 us
    all_to_all x1, blocking collectives, shards(): return lax.all_to_all(result, 'tp', split_axis=0, concat_axis=1, tiled=True)  12.4 us
    dot_general x5, matrix products, attend(): jnp.einsum('qkgj,jkd->qkgd', weights, v_part, preferred_element_type=jnp....  8.13 us
    unnamed x9, local copies, waits for them, and re-layouts  5.41 us
    all_to_all x1, blocking collectives, shards(): lax.all_to_all(rotated_key_rows, 'tp', split_axis=1, concat_axis=0, tiled...  4.44 us
    all_to_all x1, starting transfers between devices, shards(): lax.all_to_all(unscaled_value_rows, 'tp', split_axis=1, concat_axis=0, ti...  4 us
    all_to_all x1, starting transfers between devices, shards(): lax.all_to_all(queries, 'tp', split_axis=1, concat_axis=0, tiled=True)  3.59 us
  transfers between devices with their start and end apart: 18, of which 10 were waited for; matrix products, arithmetic and copies ran while one was open for 13% of the time, Pallas kernels for 0%

commit v1 on v0

v1 whole, which is shorter than its diff:
```python
import math

import jax
import jax.numpy as jnp
from jax import lax
from jax.experimental import pallas as pl
from jax.experimental.pallas import tpu as pltpu
from jax.sharding import PartitionSpec as P

CHUNKS = 4
COLUMNS = 4
MASKED = -1e30


def relays(role, slot, chunk):
    early = chunk < CHUNKS // 2
    out = []
    if slot == 4:
        if role in (2, 3) or (role == 1 and early):
            out.append(("left", 3))
        if role == 3:
            out.append(("right", 1))
    if slot == 1:
        if early and role in (0, 1, 2):
            out.append(("right", 2))
        if role == 3 and not early:
            out.append(("next_row", 5))
    if slot == 3:
        if (role == 1 and early) or (role in (2, 3) and not early):
            out.append(("left", 2))
    if slot == 5:
        if role == 0:
            out.extend([("left", 2), ("next_row", 3)])
        if role == 3:
            out.append(("right", 2))
    return out


def first_sends(role, chunk):
    out = []
    if role == 0:
        out.append(("left", 3))
    if role == 1 and chunk >= CHUNKS // 2:
        out.append(("left", 5))
    if role in (0, 1, 2):
        out.append(("right", 1))
    return out


EARLY = [3.0, 4.4, 5.8, 7.2]
EXPECTED = {
    0: {4: EARLY, 5: [None, None, 3.0, 4.4], 3: [6.0, 7.4, 8.6, 10.0], 1: [6.0, 7.4, 8.8, 10.2],
        2: [9.0, 10.4, 11.8, 13.2]},
    1: {4: EARLY, 1: EARLY, 3: [6.0, 7.4, 8.8, 10.2], 2: [9.0, 10.4, 11.8, 13.2]},
    2: {4: EARLY, 1: EARLY, 3: [6.0, 7.4, 8.8, 10.2], 2: [8.6, 10.0, 11.6, 13.0]},
    3: {4: EARLY, 1: EARLY, 3: EARLY, 5: [None, None, 8.8, 10.2], 2: [8.6, 10.0, 8.6, 10.0]},
}


def kernel(
    q_hbm, k_hbm, v_hbm, sc_hbm, len_ref, o_ref,
    kvb, qb, qs, kvf, scf, bias, top, total, acc,
    lsem, ssem, rsem, fsem,
):
    ctx, c = lax.axis_index("ctx"), lax.axis_index("tp")
    count = lax.axis_size("ctx")
    x = lax.rem(ctx, COLUMNS)
    row = ctx - x
    half_tokens, kv_heads, group, width = qb.shape[0], qb.shape[1], qb.shape[2], qb.shape[3]
    block = 2 * half_tokens
    piece = half_tokens // CHUNKS
    rows = half_tokens * group
    where = {
        "partner": (ctx, 1 - c),
        "right": (row + lax.rem(x + 1, COLUMNS), c),
        "left": (row + lax.rem(x + COLUMNS - 1, COLUMNS), c),
        "next_row": (lax.rem(ctx + COLUMNS, count), c),
    }
    last_row = (lax.rem(ctx + count - COLUMNS, count), c)

    def part(slot, half, j):
        if j == 0:
            return kvb.at[slot, half, pl.ds(0, 2 * piece + 1)]
        return kvb.at[slot, half, pl.ds(1 + 2 * piece * j, 2 * piece)]

    staged = [[] for _ in range(CHUNKS)]
    staged[0].append(pltpu.make_async_copy(sc_hbm, kvb.at[0, c, pl.ds(0, 1)], lsem.at[0]))
    for j in range(CHUNKS):
        at = 1 + 2 * piece * j
        source = pl.ds(piece * j, piece)
        staged[j].append(
            pltpu.make_async_copy(k_hbm.at[source], kvb.at[0, c, pl.ds(at, piece)], lsem.at[1 + 2 * j])
        )
        staged[j].append(
            pltpu.make_async_copy(
                v_hbm.at[source], kvb.at[0, c, pl.ds(at + piece, piece)], lsem.at[2 + 2 * j]
            )
        )
    for copies in staged:
        for copy in copies:
            copy.start()
    q_copy = pltpu.make_async_copy(q_hbm, qb, lsem.at[1 + 2 * CHUNKS])
    q_copy.start()

    barrier = pltpu.get_barrier_semaphore()
    others = list(where.values()) + [last_row]
    for other in others:
        pl.semaphore_signal(barrier, inc=1, device_id=other, device_id_type=pl.DeviceIdType.MESH)
    pl.semaphore_wait(barrier, len(others))

    counter = [0]
    open_common = []
    open_role = {r: [] for r in range(COLUMNS)}

    def remote(src, dst, send, recv, to):
        return pltpu.make_async_remote_copy(
            src_ref=src, dst_ref=dst, send_sem=ssem.at[send], recv_sem=recv,
            device_id=where[to], device_id_type=pl.DeviceIdType.MESH,
        )

    def outgoing(slot, j, to, there, number):
        recv = fsem.at[there, j] if to == "partner" else rsem.at[there, j]
        return remote(part(slot, c, j), part(there, c, j), number, recv, to)

    def send(slot, j, to, there, opened):
        sent = (slot, j, to, there, counter[0])
        counter[0] += 1
        outgoing(*sent).start()
        opened.append(sent)

    for j in range(CHUNKS):
        for copy in staged[j]:
            copy.wait()
        send(0, j, "next_row", 4, open_common)
        after_common = counter[0]
        for r in range(COLUMNS):
            counter[0] = after_common

            @pl.when(x == r)
            def _(r=r, j=j):
                for to, there in first_sends(r, j):
                    send(0, j, to, there, open_role[r])

        counter[0] = after_common + 2
        send(0, j, "partner", 0, open_common)

    order = {}
    for r in range(COLUMNS):
        events = [
            (times[j], slot, j)
            for slot, times in EXPECTED[r].items()
            for j in range(CHUNKS)
            if times[j] is not None
        ]
        order[r] = sorted(events)

    def came_in(since, until):
        first = counter[0]
        most = first
        for r in range(COLUMNS):
            counter[0] = first

            @pl.when(x == r)
            def _(r=r):
                for time, slot, j in order[r]:
                    if not since <= time < until:
                        continue
                    there = part(slot, c, j)
                    remote(there, there, 0, rsem.at[slot, j], "partner").wait_recv()
                    for to, target in relays(r, slot, j):
                        send(slot, j, to, target, open_role[r])
                    if slot != 5:
                        send(slot, j, "partner", slot, open_role[r])

            most = max(most, counter[0])
        counter[0] = most

    def other_half(slot):
        for j in range(CHUNKS):
            there = part(slot, 1 - c, j)
            remote(there, there, 0, fsem.at[slot, j], "partner").wait_recv()

    def unpack(slot):
        for half in range(2):
            scf[slot, pl.ds(kv_heads * half, kv_heads), :] = kvb[slot, half, 0].astype(jnp.float32)
            for j in range(CHUNKS):
                at = 1 + 2 * piece * j
                to = pl.ds((half_tokens * half + piece * j) * kv_heads, piece * kv_heads)
                for which in range(2):
                    tile = kvb[slot, half, pl.ds(at + which * piece, piece)].astype(jnp.float32)
                    kvf[slot, which, to, :] = tile.reshape(piece * kv_heads, width)

    ones = jnp.ones((block, width), jnp.bfloat16)
    heads_per_core = kv_heads // 2
    factor = math.log2(math.e) / math.sqrt(width)

    def attend(slots, low, high, first=False, last=False):
        @pl.loop(low, high)
        def _(h):
            q = qs[h]
            scale_row = kv_heads * (h // heads_per_core) + lax.rem(h, heads_per_core)
            scores = []
            for s in slots:
                k = kvf[s, 0, pl.ds(h, block, stride=kv_heads), :].astype(jnp.bfloat16)
                raw = lax.dot_general(
                    q, k, (((1,), (1,)), ((), ())), preferred_element_type=jnp.float32
                )
                key_scale = scf[s, pl.ds(scale_row, 1), :] * factor
                scores.append(raw * key_scale + bias[s])
            high_score = scores[0]
            for more in scores[1:]:
                high_score = jnp.maximum(high_score, more)
            new_top = jnp.broadcast_to(jnp.max(high_score, axis=1, keepdims=True), (rows, width))
            if first:
                sums = summed = None
            else:
                old = top[h]
                new_top = jnp.maximum(new_top, old)
                shrink = jnp.exp2(old - new_top)
                sums = total[h] * shrink
                summed = acc[h] * shrink
            for s, score in zip(slots, scores):
                expo = jnp.exp2(score - new_top).astype(jnp.bfloat16)
                v = kvf[s, 1, pl.ds(h, block, stride=kv_heads), :].astype(jnp.bfloat16)
                both = jnp.dot(
                    expo, jnp.concatenate([v, ones], axis=1), preferred_element_type=jnp.float32
                )
                value_scale = scf[s, pl.ds(scale_row + heads_per_core, 1), :]
                added = both[:, :width] * value_scale
                summed = added if summed is None else summed + added
                sums = both[:, width:] if sums is None else sums + both[:, width:]
            if last:
                o_ref[:, h] = (summed / sums).reshape(half_tokens, group, width).astype(o_ref.dtype)
            else:
                top[h] = new_top
                total[h] = sums
                acc[h] = summed

    lengths = jnp.broadcast_to(len_ref[...].astype(jnp.float32), (8, len_ref.shape[1]))
    docs = len_ref.shape[1]
    upto = lax.broadcasted_iota(jnp.int32, (docs, docs), 0) <= lax.broadcasted_iota(
        jnp.int32, (docs, docs), 1
    )
    ends = jnp.dot(
        lengths, upto.astype(jnp.float32), precision=lax.Precision.HIGHEST,
        preferred_element_type=jnp.float32,
    )[0:1, :]
    offset = lax.broadcasted_iota(jnp.int32, (rows, docs), 0) // group
    here = (ctx * block + c * half_tokens + offset).astype(jnp.float32)
    start = jnp.max(jnp.where(ends <= here, ends, 0.0), axis=1, keepdims=True)
    lane = lax.broadcasted_iota(jnp.int32, (rows, block), 1)
    position = (
        ctx * block + c * half_tokens + lax.broadcasted_iota(jnp.int32, (rows, block), 0) // group
    ).astype(jnp.float32)
    for s in range(5):
        key_position = (ctx * block - s * block + lane).astype(jnp.float32)
        allowed = (key_position >= start) & (key_position <= position)
        bias[s] = jnp.where(allowed, 0.0, MASKED)

    q_copy.wait()

    @pl.loop(0, kv_heads)
    def _(h):
        qs[h] = qb[:, h].astype(jnp.float32).reshape(rows, width).astype(jnp.bfloat16)

    middle = kv_heads // 2
    other_half(0)
    unpack(0)
    came_in(0.0, 3.5)
    attend([0], 0, middle, first=True)
    came_in(3.5, 5.0)
    attend([0], middle, kv_heads, first=True)
    came_in(5.0, 7.3)
    other_half(4)
    unpack(4)
    attend([4], 0, middle)
    came_in(7.3, 8.7)
    attend([4], middle, kv_heads)
    came_in(8.7, 10.3)
    other_half(1)
    other_half(3)
    unpack(1)
    unpack(3)
    attend([1, 3], 0, middle)
    came_in(10.3, 12.0)
    attend([1, 3], middle, kv_heads)
    came_in(12.0, 99.0)
    other_half(2)
    unpack(2)
    attend([2], 0, kv_heads, last=True)

    for sent in open_common:
        outgoing(*sent).wait_send()
    for r in range(COLUMNS):

        @pl.when(x == r)
        def _(r=r):
            for sent in open_role[r]:
                outgoing(*sent).wait_send()


def shards(
    queries, rotated_key_rows, unscaled_value_rows, key_block_scales, value_block_scales, doc_lengths
):
    tokens, heads, width = queries.shape
    kv_heads = rotated_key_rows.shape[1]
    group = heads // kv_heads
    rows = tokens * group
    scales = jnp.concatenate([key_block_scales, value_block_scales], axis=1)
    scales = jnp.broadcast_to(scales[:, :, None], (1, kv_heads, width))
    any_space = pl.BlockSpec(memory_space=pl.ANY)
    vmem = pl.BlockSpec(memory_space=pltpu.VMEM)
    out = pl.pallas_call(
        kernel,
        out_shape=jax.ShapeDtypeStruct((tokens, kv_heads, group, width), jnp.bfloat16),
        in_specs=[any_space] * 4 + [vmem],
        out_specs=vmem,
        scratch_shapes=[
            pltpu.VMEM((6, 2, 2 * tokens + 1, kv_heads, width), jnp.bfloat16),
            pltpu.VMEM((tokens, kv_heads, group, width), jnp.bfloat16),
            pltpu.VMEM((kv_heads, rows, width), jnp.bfloat16),
            pltpu.VMEM((5, 2, 2 * tokens * kv_heads, width), jnp.float32),
            pltpu.VMEM((5, 2 * kv_heads, width), jnp.float32),
            pltpu.VMEM((5, rows, 2 * tokens), jnp.float32),
            pltpu.VMEM((kv_heads, rows, width), jnp.float32),
            pltpu.VMEM((kv_heads, rows, width), jnp.float32),
            pltpu.VMEM((kv_heads, rows, width), jnp.float32),
            pltpu.SemaphoreType.DMA((2 + 2 * CHUNKS,)),
            pltpu.SemaphoreType.DMA((100,)),
            pltpu.SemaphoreType.DMA((6, CHUNKS)),
            pltpu.SemaphoreType.DMA((5, CHUNKS)),
        ],
        compiler_params=pltpu.CompilerParams(
            collective_id=0, has_side_effects=True, vmem_limit_bytes=60 * 1024 * 1024
        ),
    )(
        queries.reshape(tokens, kv_heads, group, width),
        rotated_key_rows,
        unscaled_value_rows,
        scales,
        doc_lengths.reshape(1, -1),
    )
    return out.reshape(tokens, heads, width)


def solution(mesh):
    return jax.shard_map(
        shards,
        mesh=mesh,
        in_specs=(
            P(("ctx", "tp"), None, None),
            P(("ctx", "tp"), None, None),
            P(("ctx", "tp"), None, None),
            P("ctx", "tp"),
            P("ctx", "tp"),
            P(),
        ),
        out_specs=P(("ctx", "tp"), None, None),
        check_vma=False,
    )
```

time: 127 us -> 46.6 us (0.37)
  the two profiles are of different devices: /device:TPU:257 before, /device:TPU:1 now
where the time goes in v1:
time: 46.6 us; the launch traced here: 46.4 us
  Pallas kernels  42.7 us (92%)
  local copies, waits for them, and re-layouts  3.58 us (8%)
    pallas_call x1, Pallas kernels, shards(): pl.pallas_call(kernel, out_shape=jax.ShapeDtypeStruct((tokens, kv_heads,...  42.7 us
    unnamed x5, local copies, waits for them, and re-layouts  2.93 us

profile of v1, /device:TPU:1, one launch (start us, length us, event | category | flops | bytes accessed | tf_op | source)
XLA Modules:
  0.0 46.4 jit_solution(6242052351191411158)
XLA Ops:
  0.0 0.0 copy-start
  0.0 0.0 copy-start.1
  0.0 0.7 %copy-done = bf16[1,4]{1,0:T(2,128)(2,1)S(1)} copy-done((bf16[1,4]{1,0:T(2,128)(2,1)S(1)}, bf16[1,4]{1,0:T(2,128)(2,1)}, u32[]{:S(2)}) %copy-start) | copy-done | bytes 32
  0.7 0.0 copy-done.1
  0.7 0.1 maximum_bitcast_fusion
  0.7 0.7 %broadcast_in_dim.9.sc_hbm = bf16[1,8,128]{2,1,0:T(8,128)(2,1)} broadcast(bf16[8]{0:T(256)(128)(2,1)S(1)} %maximum_bitcast_fusion), dimensions={1} | broadcast | bytes 2064 | tf_op jit(solution)/shard_map/broadcast_in_dim | solution.py:310
  1.4 42.7 %shard_map.64 = bf16[64,8,8,128]{3,2,1,0:T(8,128)(2,1)} custom-call(bf16[64,8,8,128]{3,2,1,0:T(8,128)(2,1)} %bitcast.6, bf16[64,8,128]{2,1,0:T(8,128)(2,1)} %k_hbm.1, bf16[64,8,128]{2,1,0:T(8,128)(2,1)} %v_hbm.1, bf16[1,8,128]{2,1,0:T(8,128)(2,1)} %broadcast_in_dim.9.sc_hbm, s32[1,256]{1,0:T(1,128)} %bitcast.7), custom_call_target="tpu_custom_call" | custom-call | tf_op jit(solution)/shard_map/pallas_call | solution.py:313
  44.2 2.3 %copy.8 = bf16[64,64,128]{2,1,0:T(8,128)(2,1)} copy(bf16[64,64,128]{2,1,0:T(8,128)(2,1)} %bitcast.5) | data formatting | bytes 2097152
Async XLA Ops:
  0.0 0.7 %copy-start = (bf16[1,4]{1,0:T(2,128)(2,1)S(1)}, bf16[1,4]{1,0:T(2,128)(2,1)}, u32[]{:S(2)}) copy-start(bf16[1,4]{1,0:T(2,128)(2,1)} %param.10) | copy-start | bytes 28
  0.0 0.7 %copy-start.1 = (bf16[1,4]{1,0:T(2,128)(2,1)S(1)}, bf16[1,4]{1,0:T(2,128)(2,1)}, u32[]{:S(2)}) copy-start(bf16[1,4]{1,0:T(2,128)(2,1)} %param.9) | copy-start | bytes 28

commit v2 on v1

--- a/solution.py
+++ b/solution.py
@@ -10,6 +10,8 @@
 CHUNKS = 4
 COLUMNS = 4
 MASKED = -1e30
+HEADS_AT_ONCE = 2
+PARTS = 1
 
 
 def relays(role, slot, chunk):
@@ -195,46 +197,79 @@
     factor = math.log2(math.e) / math.sqrt(width)
 
     def attend(slots, low, high, first=False, last=False):
-        @pl.loop(low, high)
-        def _(h):
-            q = qs[h]
-            scale_row = kv_heads * (h // heads_per_core) + lax.rem(h, heads_per_core)
-            scores = []
-            for s in slots:
-                k = kvf[s, 0, pl.ds(h, block, stride=kv_heads), :].astype(jnp.bfloat16)
-                raw = lax.dot_general(
-                    q, k, (((1,), (1,)), ((), ())), preferred_element_type=jnp.float32
+        @pl.loop(low, high, step=HEADS_AT_ONCE)
+        def _(h0):
+            items = [(i, p) for i in range(HEADS_AT_ONCE) for p in range(PARTS)]
+            part_rows = rows // PARTS
+            part_tokens = half_tokens // PARTS
+
+            def scored(i, p):
+                h = h0 + i
+                at = pl.ds(p * part_rows, part_rows)
+                scale_row = kv_heads * (h // heads_per_core) + lax.rem(h, heads_per_core)
+                out = []
+                for s in slots:
+                    k = kvf[s, 0, pl.ds(h, block, stride=kv_heads), :].astype(jnp.bfloat16)
+                    raw = lax.dot_general(
+                        qs[h, at], k, (((1,), (1,)), ((), ())), preferred_element_type=jnp.float32
+                    )
+                    key_scale = scf[s, pl.ds(scale_row, 1), :] * factor
+                    out.append(raw * key_scale + bias[s, at])
+                return out
+
+            def topped(i, p, scores):
+                h = h0 + i
+                at = pl.ds(p * part_rows, part_rows)
+                high_score = scores[0]
+                for more in scores[1:]:
+                    high_score = jnp.maximum(high_score, more)
+                new_top = jnp.broadcast_to(
+                    jnp.max(high_score, axis=1, keepdims=True), (part_rows, width)
                 )
-                key_scale = scf[s, pl.ds(scale_row, 1), :] * factor
-                scores.append(raw * key_scale + bias[s])
-            high_score = scores[0]
-            for more in scores[1:]:
-                high_score = jnp.maximum(high_score, more)
-            new_top = jnp.broadcast_to(jnp.max(high_score, axis=1, keepdims=True), (rows, width))
-            if first:
+                old = None
+                if not first:
+                    old = top[h, at]
+                    new_top = jnp.maximum(new_top, old)
+                if not last:
+                    top[h, at] = new_top
+                return old, new_top, [jnp.exp2(z - new_top).astype(jnp.bfloat16) for z in scores]
+
+            def added_up(i, p, found):
+                h = h0 + i
+                at = pl.ds(p * part_rows, part_rows)
+                scale_row = kv_heads * (h // heads_per_core) + lax.rem(h, heads_per_core)
+                old, new_top, expos = found
                 sums = summed = None
-            else:
-                old = top[h]
-                new_top = jnp.maximum(new_top, old)
-                shrink = jnp.exp2(old - new_top)
-                sums = total[h] * shrink
-                summed = acc[h] * shrink
-            for s, score in zip(slots, scores):
-                expo = jnp.exp2(score - new_top).astype(jnp.bfloat16)
-                v = kvf[s, 1, pl.ds(h, block, stride=kv_heads), :].astype(jnp.bfloat16)
-                both = jnp.dot(
-                    expo, jnp.concatenate([v, ones], axis=1), preferred_element_type=jnp.float32
-                )
-                value_scale = scf[s, pl.ds(scale_row + heads_per_core, 1), :]
-                added = both[:, :width] * value_scale
-                summed = added if summed is None else summed + added
-                sums = both[:, width:] if sums is None else sums + both[:, width:]
-            if last:
-                o_ref[:, h] = (summed / sums).reshape(half_tokens, group, width).astype(o_ref.dtype)
-            else:
-                top[h] = new_top
-                total[h] = sums
-                acc[h] = summed
+                if not first:
+                    shrink = jnp.exp2(old - new_top)
+                    sums = total[h, at] * shrink
+                    summed = acc[h, at] * shrink
+                for s, expo in zip(slots, expos):
+                    v = kvf[s, 1, pl.ds(h, block, stride=kv_heads), :].astype(jnp.bfloat16)
+                    both = jnp.dot(
+                        expo, jnp.concatenate([v, ones], axis=1), preferred_element_type=jnp.float32
+                    )
+                    value_scale = scf[s, pl.ds(scale_row + heads_per_core, 1), :]
+                    added = both[:, :width] * value_scale
+                    summed = added if summed is None else summed + added
+                    sums = both[:, width:] if sums is None else sums + both[:, width:]
+                if last:
+                    tokens = pl.ds(p * part_tokens, part_tokens)
+                    o_ref[tokens, h] = (
+                        (summed / sums).reshape(part_tokens, group, width).astype(o_ref.dtype)
+                    )
+                else:
+                    total[h, at] = sums
+                    acc[h, at] = summed
+
+            scores, found = {}, {}
+            for n in range(len(items) + 2):
+                if n < len(items):
+                    scores[n] = scored(*items[n])
+                if 0 <= n - 1 < len(items):
+                    found[n - 1] = topped(*items[n - 1], scores.pop(n - 1))
+                if 0 <= n - 2:
+                    added_up(*items[n - 2], found.pop(n - 2))
 
     lengths = jnp.broadcast_to(len_ref[...].astype(jnp.float32), (8, len_ref.shape[1]))
     docs = len_ref.shape[1]
@@ -308,7 +343,7 @@
     rows = tokens * group
     scales = jnp.concatenate([key_block_scales, value_block_scales], axis=1)
     scales = jnp.broadcast_to(scales[:, :, None], (1, kv_heads, width))
-    any_space = pl.BlockSpec(memory_space=pl.ANY)
+    any_space = pl.BlockSpec(memory_space=pltpu.HBM)
     vmem = pl.BlockSpec(memory_space=pltpu.VMEM)
     out = pl.pallas_call(
         kernel,
@@ -331,7 +366,7 @@
             pltpu.SemaphoreType.DMA((5, CHUNKS)),
         ],
         compiler_params=pltpu.CompilerParams(
-            collective_id=0, has_side_effects=True, vmem_limit_bytes=60 * 1024 * 1024
+            collective_id=0, has_side_effects=True, vmem_limit_bytes=24 * 1024 * 1024
         ),
     )(
         queries.reshape(tokens, kv_heads, group, width),

time: 46.6 us -> 42.8 us (0.918)
  Pallas kernels: 42.7 us -> 37.1 us
  local copies, waits for them, and re-layouts: 3.58 us -> 5.35 us
    pallas_call x1, Pallas kernels: 42.7 us -> 37.1 us  [shards(): pl.pallas_call(kernel, out_shape=jax.ShapeDtypeStruct((tokens, kv_heads,...]
    unnamed x5 -> x13, local copies, waits for them, and re-layouts: 2.93 us -> 5.28 us
    broadcast_in_dim x1, local copies, waits for them, and re-layouts: 0.65 us -> 0.07 us  [shards(): scales = jnp.broadcast_to(scales[:, :, None], (1, kv_heads, width))]
where the time goes in v2:
time: 42.8 us; the launch traced here: 42.6 us
  Pallas kernels  37.1 us (87%)
  local copies, waits for them, and re-layouts  5.35 us (12%)
    pallas_call x1, Pallas kernels, shards(): pl.pallas_call(kernel, out_shape=jax.ShapeDtypeStruct((tokens, kv_heads,...  37.1 us
    unnamed x13, local copies, waits for them, and re-layouts  5.28 us

profile of v2, /device:TPU:1, one launch (start us, length us, event | category | flops | bytes accessed | tf_op | source)
XLA Modules:
  0.0 42.6 jit_solution(6325898233574143505)
XLA Ops:
  0.0 0.0 copy-start.4
  0.0 0.0 copy-start.5
  0.0 0.7 %copy-done.4 = bf16[1,4]{1,0:T(2,128)(2,1)S(1)} copy-done((bf16[1,4]{1,0:T(2,128)(2,1)S(1)}, bf16[1,4]{1,0:T(2,128)(2,1)}, u32[]{:S(2)}) %copy-start.4) | copy-done | bytes 32
  0.7 0.0 copy-done.5
  0.7 0.1 maximum_bitcast_fusion
  0.7 0.0 copy-start.3
  0.8 0.1 broadcast_in_dim.9.sc_hbm
  0.8 0.6 %copy-done.3 = s32[256]{0:T(256)S(1)} copy-done((s32[256]{0:T(256)S(1)}, s32[256]{0:T(256)}, u32[]{:S(2)}) %copy-start.3) | copy-done | bytes 1048
  1.4 0.0 copy-start
  1.4 1.2 %copy-done = bf16[64,64,128]{2,1,0:T(8,128)(2,1)S(1)} copy-done((bf16[64,64,128]{2,1,0:T(8,128)(2,1)S(1)}, bf16[64,64,128]{2,1,0:T(8,128)(2,1)}, u32[]{:S(2)}) %copy-start) | copy-done | bytes 1048600
  2.7 0.0 copy-start.1
  2.7 0.9 %copy-done.1 = bf16[64,8,128]{2,1,0:T(8,128)(2,1)S(1)} copy-done((bf16[64,8,128]{2,1,0:T(8,128)(2,1)S(1)}, bf16[64,8,128]{2,1,0:T(8,128)(2,1)}, u32[]{:S(2)}) %copy-start.1) | copy-done | bytes 131096
  3.6 0.0 copy-start.2
  3.6 0.9 %copy-done.2 = bf16[64,8,128]{2,1,0:T(8,128)(2,1)S(1)} copy-done((bf16[64,8,128]{2,1,0:T(8,128)(2,1)S(1)}, bf16[64,8,128]{2,1,0:T(8,128)(2,1)}, u32[]{:S(2)}) %copy-start.2) | copy-done | bytes 131096
  4.5 37.1 %shard_map.64 = bf16[64,8,8,128]{3,2,1,0:T(8,128)(2,1)S(1)} custom-call(bf16[64,8,8,128]{3,2,1,0:T(8,128)(2,1)S(1)} %bitcast.6, bf16[64,8,128]{2,1,0:T(8,128)(2,1)S(1)} %copy-done.1, bf16[64,8,128]{2,1,0:T(8,128)(2,1)S(1)} %copy-done.2, bf16[1,8,128]{2,1,0:T(8,128)(2,1)S(1)} %broadcast_in_dim.9.sc_hbm, s32[1,256]{1,0:T(1,128)S(1)} %bitcast.7), custom_call_target="tpu_custom_call" | custom-call | tf_op jit(solution)/shard_map/pallas_call | solution.py:348
  41.6 1.0 %copy.8 = bf16[64,64,128]{2,1,0:T(8,128)(2,1)} copy(bf16[64,64,128]{2,1,0:T(8,128)(2,1)S(1)} %bitcast.5) | data formatting | bytes 2097152
Async XLA Ops:
  0.0 0.7 %copy-start.4 = (bf16[1,4]{1,0:T(2,128)(2,1)S(1)}, bf16[1,4]{1,0:T(2,128)(2,1)}, u32[]{:S(2)}) copy-start(bf16[1,4]{1,0:T(2,128)(2,1)} %param.10) | copy-start | bytes 28
  0.0 0.7 %copy-start.5 = (bf16[1,4]{1,0:T(2,128)(2,1)S(1)}, bf16[1,4]{1,0:T(2,128)(2,1)}, u32[]{:S(2)}) copy-start(bf16[1,4]{1,0:T(2,128)(2,1)} %param.9) | copy-start | bytes 28
  0.7 0.7 %copy-start.3 = (s32[256]{0:T(256)S(1)}, s32[256]{0:T(256)}, u32[]{:S(2)}) copy-start(s32[256]{0:T(256)} %param.11) | copy-start | bytes 3076
  1.4 1.2 %copy-start = (bf16[64,64,128]{2,1,0:T(8,128)(2,1)S(1)}, bf16[64,64,128]{2,1,0:T(8,128)(2,1)}, u32[]{:S(2)}) copy-start(bf16[64,64,128]{2,1,0:T(8,128)(2,1)} %param.6) | copy-start | bytes 3145732
  2.7 0.9 %copy-start.1 = (bf16[64,8,128]{2,1,0:T(8,128)(2,1)S(1)}, bf16[64,8,128]{2,1,0:T(8,128)(2,1)}, u32[]{:S(2)}) copy-start(bf16[64,8,128]{2,1,0:T(8,128)(2,1)} %k_hbm.1) | copy-start | bytes 393220
  3.6 0.9 %copy-start.2 = (bf16[64,8,128]{2,1,0:T(8,128)(2,1)S(1)}, bf16[64,8,128]{2,1,0:T(8,128)(2,1)}, u32[]{:S(2)}) copy-start(bf16[64,8,128]{2,1,0:T(8,128)(2,1)} %v_hbm.1) | copy-start | bytes 393220

commit v3 on v2

--- a/solution.py
+++ b/solution.py
@@ -60,8 +60,8 @@
 
 
 def kernel(
-    q_hbm, k_hbm, v_hbm, sc_hbm, len_ref, o_ref,
-    kvb, qb, qs, kvf, scf, bias, top, total, acc,
+    q_hbm, k_hbm, v_hbm, sc_hbm, len_hbm, o_ref,
+    len_ref, kvb, qb, qs, kvf, scf, bias, top, total, acc,
     lsem, ssem, rsem, fsem,
 ):
     ctx, c = lax.axis_index("ctx"), lax.axis_index("tp")
@@ -103,6 +103,8 @@
             copy.start()
     q_copy = pltpu.make_async_copy(q_hbm, qb, lsem.at[1 + 2 * CHUNKS])
     q_copy.start()
+    len_copy = pltpu.make_async_copy(len_hbm, len_ref, lsem.at[2 + 2 * CHUNKS])
+    len_copy.start()
 
     barrier = pltpu.get_barrier_semaphore()
     others = list(where.values()) + [last_row]
@@ -271,6 +273,7 @@
                 if 0 <= n - 2:
                     added_up(*items[n - 2], found.pop(n - 2))
 
+    len_copy.wait()
     lengths = jnp.broadcast_to(len_ref[...].astype(jnp.float32), (8, len_ref.shape[1]))
     docs = len_ref.shape[1]
     upto = lax.broadcasted_iota(jnp.int32, (docs, docs), 0) <= lax.broadcasted_iota(
@@ -343,14 +346,15 @@
     rows = tokens * group
     scales = jnp.concatenate([key_block_scales, value_block_scales], axis=1)
     scales = jnp.broadcast_to(scales[:, :, None], (1, kv_heads, width))
-    any_space = pl.BlockSpec(memory_space=pltpu.HBM)
+    in_place = pl.BlockSpec(memory_space=pltpu.HBM)
     vmem = pl.BlockSpec(memory_space=pltpu.VMEM)
     out = pl.pallas_call(
         kernel,
         out_shape=jax.ShapeDtypeStruct((tokens, kv_heads, group, width), jnp.bfloat16),
-        in_specs=[any_space] * 4 + [vmem],
+        in_specs=[in_place] * 5,
         out_specs=vmem,
         scratch_shapes=[
+            pltpu.VMEM((1, doc_lengths.shape[0]), jnp.int32),
             pltpu.VMEM((6, 2, 2 * tokens + 1, kv_heads, width), jnp.bfloat16),
             pltpu.VMEM((tokens, kv_heads, group, width), jnp.bfloat16),
             pltpu.VMEM((kv_heads, rows, width), jnp.bfloat16),
@@ -360,7 +364,7 @@
             pltpu.VMEM((kv_heads, rows, width), jnp.float32),
             pltpu.VMEM((kv_heads, rows, width), jnp.float32),
             pltpu.VMEM((kv_heads, rows, width), jnp.float32),
-            pltpu.SemaphoreType.DMA((2 + 2 * CHUNKS,)),
+            pltpu.SemaphoreType.DMA((3 + 2 * CHUNKS,)),
             pltpu.SemaphoreType.DMA((100,)),
             pltpu.SemaphoreType.DMA((6, CHUNKS)),
             pltpu.SemaphoreType.DMA((5, CHUNKS)),
@@ -369,11 +373,11 @@
             collective_id=0, has_side_effects=True, vmem_limit_bytes=24 * 1024 * 1024
         ),
     )(
-        queries.reshape(tokens, kv_heads, group, width),
-        rotated_key_rows,
-        unscaled_value_rows,
+        pltpu.with_memory_space_constraint(queries.reshape(tokens, kv_heads, group, width), pltpu.HBM),
+        pltpu.with_memory_space_constraint(rotated_key_rows, pltpu.HBM),
+        pltpu.with_memory_space_constraint(unscaled_value_rows, pltpu.HBM),
         scales,
-        doc_lengths.reshape(1, -1),
+        pltpu.with_memory_space_constraint(doc_lengths.reshape(1, -1), pltpu.HBM),
     )
     return out.reshape(tokens, heads, width)
 

time: 42.8 us -> 38.7 us (0.904)
  local copies, waits for them, and re-layouts: 5.35 us -> 1.72 us
    unnamed x13 -> x5, local copies, waits for them, and re-layouts: 5.28 us -> 1.64 us
where the time goes in v3:
time: 38.7 us; the launch traced here: 38.6 us
  Pallas kernels  36.8 us (95%)
  local copies, waits for them, and re-layouts  1.72 us (4%)
    pallas_call x1, Pallas kernels, shards(): pl.pallas_call(kernel, out_shape=jax.ShapeDtypeStruct((tokens, kv_heads,...  36.8 us
    unnamed x5, local copies, waits for them, and re-layouts  1.64 us

profile of v3, /device:TPU:1, one launch (start us, length us, event | category | flops | bytes accessed | tf_op | source)
XLA Modules:
  0.0 38.6 jit_solution(4214974221970399409)
XLA Ops:
  0.0 0.0 copy-start
  0.0 0.0 copy-start.1
  0.0 0.7 %copy-done = bf16[1,4]{1,0:T(2,128)(2,1)S(1)} copy-done((bf16[1,4]{1,0:T(2,128)(2,1)S(1)}, bf16[1,4]{1,0:T(2,128)(2,1)}, u32[]{:S(2)}) %copy-start) | copy-done | bytes 32
  0.7 0.0 copy-done.1
  0.7 0.1 maximum_bitcast_fusion
  0.7 0.1 broadcast_in_dim.9.sc_hbm
  0.8 36.8 %shard_map.64 = bf16[64,8,8,128]{3,2,1,0:T(8,128)(2,1)S(1)} custom-call(bf16[64,8,8,128]{3,2,1,0:T(8,128)(2,1)} %bitcast.6, bf16[64,8,128]{2,1,0:T(8,128)(2,1)} %k_hbm.1, bf16[64,8,128]{2,1,0:T(8,128)(2,1)} %v_hbm.1, bf16[1,8,128]{2,1,0:T(8,128)(2,1)S(1)} %broadcast_in_dim.9.sc_hbm, s32[1,256]{1,0:T(1,128)} %bitcast.7), custom_call_target="tpu_custom_call" | custom-call | tf_op jit(solution)/shard_map/pallas_call | solution.py:351
  37.6 1.0 %copy.8 = bf16[64,64,128]{2,1,0:T(8,128)(2,1)} copy(bf16[64,64,128]{2,1,0:T(8,128)(2,1)S(1)} %bitcast.5) | data formatting | bytes 2097152
Async XLA Ops:
  0.0 0.7 %copy-start = (bf16[1,4]{1,0:T(2,128)(2,1)S(1)}, bf16[1,4]{1,0:T(2,128)(2,1)}, u32[]{:S(2)}) copy-start(bf16[1,4]{1,0:T(2,128)(2,1)} %param.10) | copy-start | bytes 28
  0.0 0.7 %copy-start.1 = (bf16[1,4]{1,0:T(2,128)(2,1)S(1)}, bf16[1,4]{1,0:T(2,128)(2,1)}, u32[]{:S(2)}) copy-start(bf16[1,4]{1,0:T(2,128)(2,1)} %param.9) | copy-start | bytes 28

commit v4 on v3

--- a/solution.py
+++ b/solution.py
@@ -11,7 +11,6 @@
 COLUMNS = 4
 MASKED = -1e30
 HEADS_AT_ONCE = 2
-PARTS = 1
 
 
 def relays(role, slot, chunk):
@@ -194,104 +193,100 @@
                     tile = kvb[slot, half, pl.ds(at + which * piece, piece)].astype(jnp.float32)
                     kvf[slot, which, to, :] = tile.reshape(piece * kv_heads, width)
 
-    ones = jnp.ones((block, width), jnp.bfloat16)
     heads_per_core = kv_heads // 2
     factor = math.log2(math.e) / math.sqrt(width)
 
-    def attend(slots, low, high, first=False, last=False):
+    def attend(slots, before, low, high, last=False):
+        first = before is None
+
         @pl.loop(low, high, step=HEADS_AT_ONCE)
         def _(h0):
-            items = [(i, p) for i in range(HEADS_AT_ONCE) for p in range(PARTS)]
-            part_rows = rows // PARTS
-            part_tokens = half_tokens // PARTS
-
-            def scored(i, p):
+            def scale(s, h, which):
+                at = kv_heads * (h // heads_per_core) + lax.rem(h, heads_per_core)
+                one = scf[s, pl.ds(at + which * heads_per_core, 1), :]
+                return jnp.concatenate([one] * (rows // width), axis=1)
+
+            def scored(i):
                 h = h0 + i
-                at = pl.ds(p * part_rows, part_rows)
-                scale_row = kv_heads * (h // heads_per_core) + lax.rem(h, heads_per_core)
                 out = []
                 for s in slots:
                     k = kvf[s, 0, pl.ds(h, block, stride=kv_heads), :].astype(jnp.bfloat16)
-                    raw = lax.dot_general(
-                        qs[h, at], k, (((1,), (1,)), ((), ())), preferred_element_type=jnp.float32
-                    )
-                    key_scale = scf[s, pl.ds(scale_row, 1), :] * factor
-                    out.append(raw * key_scale + bias[s, at])
+                    raw = jnp.dot(k, qs[h], preferred_element_type=jnp.float32)
+                    out.append(raw * (scale(s, h, 0) * factor) + bias[s])
                 return out
 
-            def topped(i, p, scores):
+            def topped(i, scores):
                 h = h0 + i
-                at = pl.ds(p * part_rows, part_rows)
                 high_score = scores[0]
                 for more in scores[1:]:
                     high_score = jnp.maximum(high_score, more)
-                new_top = jnp.broadcast_to(
-                    jnp.max(high_score, axis=1, keepdims=True), (part_rows, width)
-                )
-                old = None
+                new_top = jnp.max(high_score, axis=0, keepdims=True)
+                sums = shrink = None
                 if not first:
-                    old = top[h, at]
+                    old = top[h]
                     new_top = jnp.maximum(new_top, old)
+                    shrink = jnp.exp2(old - new_top)
+                    sums = total[h] * shrink
                 if not last:
-                    top[h, at] = new_top
-                return old, new_top, [jnp.exp2(z - new_top).astype(jnp.bfloat16) for z in scores]
-
-            def added_up(i, p, found):
+                    top[h] = new_top
+                expos = []
+                for score in scores:
+                    expo = jnp.exp2(score - new_top)
+                    added = jnp.sum(expo, axis=0, keepdims=True)
+                    sums = added if sums is None else sums + added
+                    expos.append(expo.astype(jnp.bfloat16))
+                return sums, shrink, expos
+
+            def added_up(i, found):
                 h = h0 + i
-                at = pl.ds(p * part_rows, part_rows)
-                scale_row = kv_heads * (h // heads_per_core) + lax.rem(h, heads_per_core)
-                old, new_top, expos = found
-                sums = summed = None
-                if not first:
-                    shrink = jnp.exp2(old - new_top)
-                    sums = total[h, at] * shrink
-                    summed = acc[h, at] * shrink
+                sums, shrink, expos = found
+                summed = None if first else acc[h]
+                unit = None if first else scale(before, h, 1)
                 for s, expo in zip(slots, expos):
-                    v = kvf[s, 1, pl.ds(h, block, stride=kv_heads), :].astype(jnp.bfloat16)
-                    both = jnp.dot(
-                        expo, jnp.concatenate([v, ones], axis=1), preferred_element_type=jnp.float32
-                    )
-                    value_scale = scf[s, pl.ds(scale_row + heads_per_core, 1), :]
-                    added = both[:, :width] * value_scale
-                    summed = added if summed is None else summed + added
-                    sums = both[:, width:] if sums is None else sums + both[:, width:]
+                    v = kvf[s, 1, pl.ds(h, block, stride=kv_heads), :].T.astype(jnp.bfloat16)
+                    added = jnp.dot(v, expo, preferred_element_type=jnp.float32)
+                    new_unit = scale(s, h, 1)
+                    if summed is None:
+                        summed = added
+                    else:
+                        ratio = unit / new_unit
+                        if shrink is not None:
+                            ratio = ratio * shrink
+                        summed = summed * ratio + added
+                    unit, shrink = new_unit, None
                 if last:
-                    tokens = pl.ds(p * part_tokens, part_tokens)
-                    o_ref[tokens, h] = (
-                        (summed / sums).reshape(part_tokens, group, width).astype(o_ref.dtype)
-                    )
+                    result = (summed * (unit / sums)).T
+                    o_ref[:, h] = result.reshape(half_tokens, group, width).astype(o_ref.dtype)
                 else:
-                    total[h, at] = sums
-                    acc[h, at] = summed
+                    total[h] = sums
+                    acc[h] = summed
 
             scores, found = {}, {}
-            for n in range(len(items) + 2):
-                if n < len(items):
-                    scores[n] = scored(*items[n])
-                if 0 <= n - 1 < len(items):
-                    found[n - 1] = topped(*items[n - 1], scores.pop(n - 1))
+            for n in range(HEADS_AT_ONCE + 2):
+                if n < HEADS_AT_ONCE:
+                    scores[n] = scored(n)
+                if 0 <= n - 1 < HEADS_AT_ONCE:
+                    found[n - 1] = topped(n - 1, scores.pop(n - 1))
                 if 0 <= n - 2:
-                    added_up(*items[n - 2], found.pop(n - 2))
+                    added_up(n - 2, found.pop(n - 2))
 
     len_copy.wait()
     lengths = jnp.broadcast_to(len_ref[...].astype(jnp.float32), (8, len_ref.shape[1]))
     docs = len_ref.shape[1]
-    upto = lax.broadcasted_iota(jnp.int32, (docs, docs), 0) <= lax.broadcasted_iota(
-        jnp.int32, (docs, docs), 1
+    upto = lax.broadcasted_iota(jnp.int32, (docs, docs), 1) <= lax.broadcasted_iota(
+        jnp.int32, (docs, docs), 0
     )
-    ends = jnp.dot(
-        lengths, upto.astype(jnp.float32), precision=lax.Precision.HIGHEST,
-        preferred_element_type=jnp.float32,
-    )[0:1, :]
-    offset = lax.broadcasted_iota(jnp.int32, (rows, docs), 0) // group
-    here = (ctx * block + c * half_tokens + offset).astype(jnp.float32)
-    start = jnp.max(jnp.where(ends <= here, ends, 0.0), axis=1, keepdims=True)
-    lane = lax.broadcasted_iota(jnp.int32, (rows, block), 1)
-    position = (
-        ctx * block + c * half_tokens + lax.broadcasted_iota(jnp.int32, (rows, block), 0) // group
-    ).astype(jnp.float32)
+    ends = lax.dot_general(
+        upto.astype(jnp.float32), lengths, (((1,), (1,)), ((), ())),
+        precision=lax.Precision.HIGHEST, preferred_element_type=jnp.float32,
+    )[:, 0:1]
+    here = ctx * block + c * half_tokens + lax.broadcasted_iota(jnp.int32, (1, rows), 1) // group
+    position = here.astype(jnp.float32)
+    start = jnp.max(jnp.where(ends <= position, ends, 0.0), axis=0, keepdims=True)
     for s in range(5):
-        key_position = (ctx * block - s * block + lane).astype(jnp.float32)
+        key_position = (
+            ctx * block - s * block + lax.broadcasted_iota(jnp.int32, (block, rows), 0)
+        ).astype(jnp.float32)
         allowed = (key_position >= start) & (key_position <= position)
         bias[s] = jnp.where(allowed, 0.0, MASKED)
 
@@ -299,33 +294,37 @@
 
     @pl.loop(0, kv_heads)
     def _(h):
-        qs[h] = qb[:, h].astype(jnp.float32).reshape(rows, width).astype(jnp.bfloat16)
+        qs[h] = qb[:, h].astype(jnp.float32).reshape(rows, width).T.astype(jnp.bfloat16)
 
     middle = kv_heads // 2
     other_half(0)
     unpack(0)
+    attend([0], None, 0, middle)
     came_in(0.0, 3.5)
-    attend([0], 0, middle, first=True)
-    came_in(3.5, 5.0)
-    attend([0], middle, kv_heads, first=True)
-    came_in(5.0, 7.3)
+    attend([0], None, middle, kv_heads)
+    came_in(3.5, 7.3)
     other_half(4)
     unpack(4)
-    attend([4], 0, middle)
-    came_in(7.3, 8.7)
-    attend([4], middle, kv_heads)
+    attend([4], 0, 0, 2)
+    came_in(7.3, 7.5)
+    attend([4], 0, 2, 6)
+    came_in(7.5, 8.7)
+    attend([4], 0, 6, kv_heads)
     came_in(8.7, 10.3)
     other_half(1)
+    unpack(1)
+    attend([1], 4, 0, middle)
+    came_in(10.3, 10.5)
+    attend([1], 4, middle, kv_heads)
     other_half(3)
-    unpack(1)
     unpack(3)
-    attend([1, 3], 0, middle)
-    came_in(10.3, 12.0)
-    attend([1, 3], middle, kv_heads)
+    attend([3], 1, 0, middle)
+    came_in(10.5, 12.0)
+    attend([3], 1, middle, kv_heads)
     came_in(12.0, 99.0)
     other_half(2)
     unpack(2)
-    attend([2], 0, kv_heads, last=True)
+    attend([2], 3, 0, kv_heads, last=True)
 
     for sent in open_common:
         outgoing(*sent).wait_send()
@@ -357,13 +356,13 @@
             pltpu.VMEM((1, doc_lengths.shape[0]), jnp.int32),
             pltpu.VMEM((6, 2, 2 * tokens + 1, kv_heads, width), jnp.bfloat16),
             pltpu.VMEM((tokens, kv_heads, group, width), jnp.bfloat16),
-            pltpu.VMEM((kv_heads, rows, width), jnp.bfloat16),
+            pltpu.VMEM((kv_heads, width, rows), jnp.bfloat16),
             pltpu.VMEM((5, 2, 2 * tokens * kv_heads, width), jnp.float32),
             pltpu.VMEM((5, 2 * kv_heads, width), jnp.float32),
-            pltpu.VMEM((5, rows, 2 * tokens), jnp.float32),
-            pltpu.VMEM((kv_heads, rows, width), jnp.float32),
-            pltpu.VMEM((kv_heads, rows, width), jnp.float32),
-            pltpu.VMEM((kv_heads, rows, width), jnp.float32),
+            pltpu.VMEM((5, 2 * tokens, rows), jnp.float32),
+            pltpu.VMEM((kv_heads, 1, rows), jnp.float32),
+            pltpu.VMEM((kv_heads, 1, rows), jnp.float32),
+            pltpu.VMEM((kv_heads, width, rows), jnp.float32),
             pltpu.SemaphoreType.DMA((3 + 2 * CHUNKS,)),
             pltpu.SemaphoreType.DMA((100,)),
             pltpu.SemaphoreType.DMA((6, CHUNKS)),

time: 38.7 us -> 39 us (level)
  no operation moved by 1% of the time
where the time goes in v4:
time: 39 us; the launch traced here: 38.9 us
  Pallas kernels  37.1 us (95%)
  local copies, waits for them, and re-layouts  1.72 us (4%)
    pallas_call x1, Pallas kernels, shards(): pl.pallas_call(kernel, out_shape=jax.ShapeDtypeStruct((tokens, kv_heads,...  37.1 us
    unnamed x5, local copies, waits for them, and re-layouts  1.64 us

profile of v4, /device:TPU:1, one launch (start us, length us, event | category | flops | bytes accessed | tf_op | source)
XLA Modules:
  0.0 38.9 jit_solution(16605191552051424313)
XLA Ops:
  0.0 0.0 copy-start
  0.0 0.0 copy-start.1
  0.0 0.7 %copy-done = bf16[1,4]{1,0:T(2,128)(2,1)S(1)} copy-done((bf16[1,4]{1,0:T(2,128)(2,1)S(1)}, bf16[1,4]{1,0:T(2,128)(2,1)}, u32[]{:S(2)}) %copy-start) | copy-done | bytes 32
  0.7 0.0 copy-done.1
  0.7 0.1 maximum_bitcast_fusion
  0.7 0.1 broadcast_in_dim.9.sc_hbm
  0.8 37.1 %shard_map.64 = bf16[64,8,8,128]{3,2,1,0:T(8,128)(2,1)S(1)} custom-call(bf16[64,8,8,128]{3,2,1,0:T(8,128)(2,1)} %bitcast.6, bf16[64,8,128]{2,1,0:T(8,128)(2,1)} %k_hbm.1, bf16[64,8,128]{2,1,0:T(8,128)(2,1)} %v_hbm.1, bf16[1,8,128]{2,1,0:T(8,128)(2,1)S(1)} %broadcast_in_dim.9.sc_hbm, s32[1,256]{1,0:T(1,128)} %bitcast.7), custom_call_target="tpu_custom_call" | custom-call | tf_op jit(solution)/shard_map/pallas_call | solution.py:350
  37.9 1.0 %copy.8 = bf16[64,64,128]{2,1,0:T(8,128)(2,1)} copy(bf16[64,64,128]{2,1,0:T(8,128)(2,1)S(1)} %bitcast.5) | data formatting | bytes 2097152
Async XLA Ops:
  0.0 0.7 %copy-start = (bf16[1,4]{1,0:T(2,128)(2,1)S(1)}, bf16[1,4]{1,0:T(2,128)(2,1)}, u32[]{:S(2)}) copy-start(bf16[1,4]{1,0:T(2,128)(2,1)} %param.10) | copy-start | bytes 28
  0.0 0.7 %copy-start.1 = (bf16[1,4]{1,0:T(2,128)(2,1)S(1)}, bf16[1,4]{1,0:T(2,128)(2,1)}, u32[]{:S(2)}) copy-start(bf16[1,4]{1,0:T(2,128)(2,1)} %param.9) | copy-start | bytes 28

commit v5 on v4

--- a/solution.py
+++ b/solution.py
@@ -106,10 +106,34 @@
     len_copy.start()
 
     barrier = pltpu.get_barrier_semaphore()
-    others = list(where.values()) + [last_row]
-    for other in others:
+    has_next = ctx < count - COLUMNS
+    has_last = ctx >= COLUMNS
+
+    def greet(other):
         pl.semaphore_signal(barrier, inc=1, device_id=other, device_id_type=pl.DeviceIdType.MESH)
-    pl.semaphore_wait(barrier, len(others))
+
+    for other in ("partner", "right", "left"):
+        greet(where[other])
+    pl.when(has_next)(lambda: greet(where["next_row"]))
+    pl.when(has_last)(lambda: greet(last_row))
+
+    def stand_in(slot, chunks):
+        for j in chunks:
+            at = 1 + 2 * piece * j
+            source = pl.ds(piece * j, piece)
+            sem = rsem.at[slot, j]
+            if j == 0:
+                pltpu.make_async_copy(sc_hbm, kvb.at[slot, c, pl.ds(0, 1)], sem).start()
+            pltpu.make_async_copy(k_hbm.at[source], kvb.at[slot, c, pl.ds(at, piece)], sem).start()
+            pltpu.make_async_copy(
+                v_hbm.at[source], kvb.at[slot, c, pl.ds(at + piece, piece)], sem
+            ).start()
+
+    late = range(CHUNKS // 2, CHUNKS)
+    pl.when(jnp.logical_not(has_last))(lambda: stand_in(4, range(CHUNKS)))
+    pl.when(ctx == 0)(lambda: stand_in(3, late))
+    pl.when(ctx == COLUMNS - 1)(lambda: stand_in(5, late))
+    pl.semaphore_wait(barrier, 3 + has_next.astype(jnp.int32) + has_last.astype(jnp.int32))
 
     counter = [0]
     open_common = []
@@ -128,8 +152,17 @@
     def send(slot, j, to, there, opened):
         sent = (slot, j, to, there, counter[0])
         counter[0] += 1
-        outgoing(*sent).start()
+        if to == "next_row":
+            pl.when(has_next)(lambda: outgoing(*sent).start())
+        else:
+            outgoing(*sent).start()
         opened.append(sent)
+
+    def finish(sent):
+        if sent[2] == "next_row":
+            pl.when(has_next)(lambda: outgoing(*sent).wait_send())
+        else:
+            outgoing(*sent).wait_send()
 
     for j in range(CHUNKS):
         for copy in staged[j]:
@@ -327,13 +360,13 @@
     attend([2], 3, 0, kv_heads, last=True)
 
     for sent in open_common:
-        outgoing(*sent).wait_send()
+        finish(sent)
     for r in range(COLUMNS):
 
         @pl.when(x == r)
         def _(r=r):
             for sent in open_role[r]:
-                outgoing(*sent).wait_send()
+                finish(sent)
 
 
 def shards(

time: 39 us -> 32 us (0.82)
  Pallas kernels: 37.1 us -> 30.1 us
    pallas_call x1, Pallas kernels: 37.1 us -> 30.1 us  [shards(): pl.pallas_call(kernel, out_shape=jax.ShapeDtypeStruct((tokens, kv_heads,...]
where the time goes in v5:
time: 32 us; the launch traced here: 31.9 us
  Pallas kernels  30.1 us (94%)
  local copies, waits for them, and re-layouts  1.72 us (5%)
    pallas_call x1, Pallas kernels, shards(): pl.pallas_call(kernel, out_shape=jax.ShapeDtypeStruct((tokens, kv_heads,...  30.1 us
    unnamed x5, local copies, waits for them, and re-layouts  1.64 us

profile of v5, /device:TPU:1, one launch (start us, length us, event | category | flops | bytes accessed | tf_op | source)
XLA Modules:
  0.0 31.9 jit_solution(4080158491461548025)
XLA Ops:
  0.0 0.0 copy-start
  0.0 0.0 copy-start.1
  0.0 0.7 %copy-done = bf16[1,4]{1,0:T(2,128)(2,1)S(1)} copy-done((bf16[1,4]{1,0:T(2,128)(2,1)S(1)}, bf16[1,4]{1,0:T(2,128)(2,1)}, u32[]{:S(2)}) %copy-start) | copy-done | bytes 32
  0.7 0.0 copy-done.1
  0.7 0.1 maximum_bitcast_fusion
  0.7 0.1 broadcast_in_dim.9.sc_hbm
  0.8 30.1 %shard_map.64 = bf16[64,8,8,128]{3,2,1,0:T(8,128)(2,1)S(1)} custom-call(bf16[64,8,8,128]{3,2,1,0:T(8,128)(2,1)} %bitcast.6, bf16[64,8,128]{2,1,0:T(8,128)(2,1)} %k_hbm.1, bf16[64,8,128]{2,1,0:T(8,128)(2,1)} %v_hbm.1, bf16[1,8,128]{2,1,0:T(8,128)(2,1)S(1)} %broadcast_in_dim.9.sc_hbm, s32[1,256]{1,0:T(1,128)} %bitcast.7), custom_call_target="tpu_custom_call" | custom-call | tf_op jit(solution)/shard_map/pallas_call | solution.py:383
  30.9 1.0 %copy.8 = bf16[64,64,128]{2,1,0:T(8,128)(2,1)} copy(bf16[64,64,128]{2,1,0:T(8,128)(2,1)S(1)} %bitcast.5) | data formatting | bytes 2097152
Async XLA Ops:
  0.0 0.7 %copy-start = (bf16[1,4]{1,0:T(2,128)(2,1)S(1)}, bf16[1,4]{1,0:T(2,128)(2,1)}, u32[]{:S(2)}) copy-start(bf16[1,4]{1,0:T(2,128)(2,1)} %param.10) | copy-start | bytes 28
  0.0 0.7 %copy-start.1 = (bf16[1,4]{1,0:T(2,128)(2,1)S(1)}, bf16[1,4]{1,0:T(2,128)(2,1)}, u32[]{:S(2)}) copy-start(bf16[1,4]{1,0:T(2,128)(2,1)} %param.9) | copy-start | bytes 28

commit v6 on v5

--- a/solution.py
+++ b/solution.py
@@ -117,27 +117,28 @@
     pl.when(has_next)(lambda: greet(where["next_row"]))
     pl.when(has_last)(lambda: greet(last_row))
 
-    def stand_in(slot, chunks):
-        for j in chunks:
+    def stand_in(slot):
+        for j in range(CHUNKS):
             at = 1 + 2 * piece * j
             source = pl.ds(piece * j, piece)
-            sem = rsem.at[slot, j]
-            if j == 0:
-                pltpu.make_async_copy(sc_hbm, kvb.at[slot, c, pl.ds(0, 1)], sem).start()
-            pltpu.make_async_copy(k_hbm.at[source], kvb.at[slot, c, pl.ds(at, piece)], sem).start()
-            pltpu.make_async_copy(
-                v_hbm.at[source], kvb.at[slot, c, pl.ds(at + piece, piece)], sem
-            ).start()
-
-    late = range(CHUNKS // 2, CHUNKS)
-    pl.when(jnp.logical_not(has_last))(lambda: stand_in(4, range(CHUNKS)))
-    pl.when(ctx == 0)(lambda: stand_in(3, late))
-    pl.when(ctx == COLUMNS - 1)(lambda: stand_in(5, late))
+            for half, sem in ((c, rsem.at[slot, j]), (1 - c, fsem.at[slot, j])):
+                if j == 0:
+                    pltpu.make_async_copy(sc_hbm, kvb.at[slot, half, pl.ds(0, 1)], sem).start()
+                pltpu.make_async_copy(
+                    k_hbm.at[source], kvb.at[slot, half, pl.ds(at, piece)], sem
+                ).start()
+                pltpu.make_async_copy(
+                    v_hbm.at[source], kvb.at[slot, half, pl.ds(at + piece, piece)], sem
+                ).start()
+
+    for slot in range(1, 5):
+        pl.when(ctx < slot)(lambda slot=slot: stand_in(slot))
     pl.semaphore_wait(barrier, 3 + has_next.astype(jnp.int32) + has_last.astype(jnp.int32))
 
     counter = [0]
     open_common = []
     open_role = {r: [] for r in range(COLUMNS)}
+    open_late = {(r, top): [] for r in range(COLUMNS) for top in (False, True)}
 
     def remote(src, dst, send, recv, to):
         return pltpu.make_async_remote_copy(
@@ -190,23 +191,30 @@
         ]
         order[r] = sorted(events)
 
+    def reach(r, to):
+        return (r + (1 if to == "right" else COLUMNS - 1)) % COLUMNS
+
     def came_in(since, until):
         first = counter[0]
         most = first
-        for r in range(COLUMNS):
+        for r, top_row in open_late:
             counter[0] = first
 
-            @pl.when(x == r)
-            def _(r=r):
+            @pl.when((x == r) & (has_last != top_row))
+            def _(r=r, top_row=top_row):
+                opened = open_late[r, top_row]
                 for time, slot, j in order[r]:
-                    if not since <= time < until:
+                    if not since <= time < until or (top_row and slot == 5 and r != 0):
                         continue
                     there = part(slot, c, j)
                     remote(there, there, 0, rsem.at[slot, j], "partner").wait_recv()
+                    if top_row and r < slot < 5:
+                        continue
                     for to, target in relays(r, slot, j):
-                        send(slot, j, to, target, open_role[r])
+                        if not (top_row and to != "next_row" and reach(r, to) < target < 5):
+                            send(slot, j, to, target, opened)
                     if slot != 5:
-                        send(slot, j, "partner", slot, open_role[r])
+                        send(slot, j, "partner", slot, opened)
 
             most = max(most, counter[0])
         counter[0] = most
@@ -366,6 +374,13 @@
         @pl.when(x == r)
         def _(r=r):
             for sent in open_role[r]:
+                finish(sent)
+
+    for r, top_row in open_late:
+
+        @pl.when((x == r) & (has_last != top_row))
+        def _(r=r, top_row=top_row):
+            for sent in open_late[r, top_row]:
                 finish(sent)
 
 

time: 32 us -> 30.3 us (0.947)
  the two profiles are of different devices: /device:TPU:1 before, /device:TPU:257 now
where the time goes in v6:
time: 30.3 us; the launch traced here: 30.2 us
  Pallas kernels  28.4 us (94%)
  local copies, waits for them, and re-layouts  1.72 us (6%)
    pallas_call x1, Pallas kernels, shards(): pl.pallas_call(kernel, out_shape=jax.ShapeDtypeStruct((tokens, kv_heads,...  28.4 us
    unnamed x5, local copies, waits for them, and re-layouts  1.64 us

profile of v6, /device:TPU:257, one launch (start us, length us, event | category | flops | bytes accessed | tf_op | source)
XLA Modules:
  0.0 30.2 jit_solution(8933103475431739159)
XLA Ops:
  0.0 0.0 copy-start
  0.0 0.0 copy-start.1
  0.0 0.7 %copy-done = bf16[1,4]{1,0:T(2,128)(2,1)S(1)} copy-done((bf16[1,4]{1,0:T(2,128)(2,1)S(1)}, bf16[1,4]{1,0:T(2,128)(2,1)}, u32[]{:S(2)}) %copy-start) | copy-done | bytes 32
  0.7 0.0 copy-done.1
  0.7 0.1 maximum_bitcast_fusion
  0.7 0.1 broadcast_in_dim.9.sc_hbm
  0.8 28.4 %shard_map.64 = bf16[64,8,8,128]{3,2,1,0:T(8,128)(2,1)S(1)} custom-call(bf16[64,8,8,128]{3,2,1,0:T(8,128)(2,1)} %bitcast.6, bf16[64,8,128]{2,1,0:T(8,128)(2,1)} %k_hbm.1, bf16[64,8,128]{2,1,0:T(8,128)(2,1)} %v_hbm.1, bf16[1,8,128]{2,1,0:T(8,128)(2,1)S(1)} %broadcast_in_dim.9.sc_hbm, s32[1,256]{1,0:T(1,128)} %bitcast.7), custom_call_target="tpu_custom_call" | custom-call | tf_op jit(solution)/shard_map/pallas_call | solution.py:398
  29.2 1.0 %copy.8 = bf16[64,64,128]{2,1,0:T(8,128)(2,1)} copy(bf16[64,64,128]{2,1,0:T(8,128)(2,1)S(1)} %bitcast.5) | data formatting | bytes 2097152
Async XLA Ops:
  0.0 0.7 %copy-start = (bf16[1,4]{1,0:T(2,128)(2,1)S(1)}, bf16[1,4]{1,0:T(2,128)(2,1)}, u32[]{:S(2)}) copy-start(bf16[1,4]{1,0:T(2,128)(2,1)} %param.10) | copy-start | bytes 28
  0.0 0.7 %copy-start.1 = (bf16[1,4]{1,0:T(2,128)(2,1)S(1)}, bf16[1,4]{1,0:T(2,128)(2,1)}, u32[]{:S(2)}) copy-start(bf16[1,4]{1,0:T(2,128)(2,1)} %param.9) | copy-start | bytes 28

commit v7 on v6

--- a/solution.py
+++ b/solution.py
@@ -7,7 +7,7 @@
 from jax.experimental.pallas import tpu as pltpu
 from jax.sharding import PartitionSpec as P
 
-CHUNKS = 4
+CHUNKS = 8
 COLUMNS = 4
 MASKED = -1e30
 HEADS_AT_ONCE = 2
@@ -181,13 +181,17 @@
         counter[0] = after_common + 2
         send(0, j, "partner", 0, open_common)
 
+    def due(times, j):
+        time = times[j * len(times) // CHUNKS]
+        return None if time is None else time - 0.7 * (1 - j % 2)
+
     order = {}
     for r in range(COLUMNS):
         events = [
-            (times[j], slot, j)
+            (due(times, j), slot, j)
             for slot, times in EXPECTED[r].items()
             for j in range(CHUNKS)
-            if times[j] is not None
+            if due(times, j) is not None
         ]
         order[r] = sorted(events)
 
@@ -412,7 +416,7 @@
             pltpu.VMEM((kv_heads, 1, rows), jnp.float32),
             pltpu.VMEM((kv_heads, width, rows), jnp.float32),
             pltpu.SemaphoreType.DMA((3 + 2 * CHUNKS,)),
-            pltpu.SemaphoreType.DMA((100,)),
+            pltpu.SemaphoreType.DMA((200,)),
             pltpu.SemaphoreType.DMA((6, CHUNKS)),
             pltpu.SemaphoreType.DMA((5, CHUNKS)),
         ],

time: 30.3 us -> 32 us (1.056)
  the two profiles are of different devices: /device:TPU:257 before, /device:TPU:9 now
where the time goes in v7:
time: 32 us; the launch traced here: 31.8 us
  Pallas kernels  30 us (94%)
  local copies, waits for them, and re-layouts  1.72 us (5%)
    pallas_call x1, Pallas kernels, shards(): pl.pallas_call(kernel, out_shape=jax.ShapeDtypeStruct((tokens, kv_heads,...  30 us
    unnamed x5, local copies, waits for them, and re-layouts  1.64 us

profile of v7, /device:TPU:9, one launch (start us, length us, event | category | flops | bytes accessed | tf_op | source)
XLA Modules:
  0.0 31.8 jit_solution(17230349831552626876)
XLA Ops:
  0.0 0.0 copy-start
  0.0 0.0 copy-start.1
  0.0 0.7 %copy-done = bf16[1,4]{1,0:T(2,128)(2,1)S(1)} copy-done((bf16[1,4]{1,0:T(2,128)(2,1)S(1)}, bf16[1,4]{1,0:T(2,128)(2,1)}, u32[]{:S(2)}) %copy-start) | copy-done | bytes 32
  0.7 0.0 copy-done.1
  0.7 0.1 maximum_bitcast_fusion
  0.7 0.1 broadcast_in_dim.9.sc_hbm
  0.8 30.0 %shard_map.64 = bf16[64,8,8,128]{3,2,1,0:T(8,128)(2,1)S(1)} custom-call(bf16[64,8,8,128]{3,2,1,0:T(8,128)(2,1)} %bitcast.6, bf16[64,8,128]{2,1,0:T(8,128)(2,1)} %k_hbm.1, bf16[64,8,128]{2,1,0:T(8,128)(2,1)} %v_hbm.1, bf16[1,8,128]{2,1,0:T(8,128)(2,1)S(1)} %broadcast_in_dim.9.sc_hbm, s32[1,256]{1,0:T(1,128)} %bitcast.7), custom_call_target="tpu_custom_call" | custom-call | tf_op jit(solution)/shard_map/pallas_call | solution.py:402
  30.8 1.0 %copy.8 = bf16[64,64,128]{2,1,0:T(8,128)(2,1)} copy(bf16[64,64,128]{2,1,0:T(8,128)(2,1)S(1)} %bitcast.5) | data formatting | bytes 2097152
Async XLA Ops:
  0.0 0.7 %copy-start = (bf16[1,4]{1,0:T(2,128)(2,1)S(1)}, bf16[1,4]{1,0:T(2,128)(2,1)}, u32[]{:S(2)}) copy-start(bf16[1,4]{1,0:T(2,128)(2,1)} %param.10) | copy-start | bytes 28
  0.0 0.7 %copy-start.1 = (bf16[1,4]{1,0:T(2,128)(2,1)S(1)}, bf16[1,4]{1,0:T(2,128)(2,1)}, u32[]{:S(2)}) copy-start(bf16[1,4]{1,0:T(2,128)(2,1)} %param.9) | copy-start | bytes 28
